TPU v7x, 512 devices: a whole 4x8x8 slice. The times are simulated.
512 devices in a mesh: row: 16 (over y, core), col: 32 (over z, x).
Axes of the slice: x: 4, y: 8, z: 8, core: 2. Of those that a mesh axis runs over, the one named last changes fastest.
Arguments:
- particles: float32 [16384, 128], P('row'), may hold values from -4 to 4
- log_weights: float32 [16384], P('row'), may hold values from -8 to 8
- targets: float32 [49152, 128], P('col'), may hold values from -5 to 5
Outputs:
- new_particles: float32 [49152, 128], P(('col', 'row'))
All inputs are finite; a program needn't handle non-finite values.
Results may differ from a plain program's by a relative error of at most 0.005.
Values sent between devices are 32-bit elements; how exact they have to be, the bound alone decides.
No kernel may reach another device: no remote copies, remote signals or barrier semaphores. Data moves between devices by JAX's collectives and lax.ppermute only.
A program may use at most 64 MiB of HBM per device.

v0:
```python
import math

import jax
import jax.numpy as jnp
from jax import lax
from jax.sharding import PartitionSpec as P

ITERS = 3


EPS = 0.01


def cost_tile(source, points):
    source_sq = jnp.sum(source * source, axis=1)
    points_sq = jnp.sum(points * points, axis=1)
    cross = jnp.dot(
        source, points.T, precision=lax.Precision.HIGHEST, preferred_element_type=jnp.float32
    )
    return (source_sq[:, None] + points_sq[None, :] - 2.0 * cross) / source.shape[1]


def row_update(particles, log_weights, targets, col_pot, block_count, block_rows):
    maxima = []
    totals = []
    for index in range(block_count):
        source = particles[index * block_rows : (index + 1) * block_rows]
        scores = (col_pot[None, :] - cost_tile(source, targets)) / EPS
        top = jnp.max(scores, axis=1)
        maxima.append(top)
        totals.append(jnp.sum(jnp.exp(scores - top[:, None]), axis=1))
    local_top = jnp.concatenate(maxima)
    local_sum = jnp.concatenate(totals)
    top = lax.pmax(local_top, "col")
    summed = lax.psum(local_sum * jnp.exp(local_top - top), "col")
    return EPS * (log_weights - (top + jnp.log(summed)))


def col_update(particles, targets, row_pot, block_count, block_rows):
    width = targets.shape[0]
    top = jnp.full((width,), -1e30, jnp.float32)
    summed = jnp.zeros((width,), jnp.float32)
    for index in range(block_count):
        source = particles[index * block_rows : (index + 1) * block_rows]
        potential = row_pot[index * block_rows : (index + 1) * block_rows]
        scores = (potential[:, None] - cost_tile(source, targets)) / EPS
        fresh = jnp.maximum(top, jnp.max(scores, axis=0))
        summed = summed * jnp.exp(top - fresh) + jnp.sum(jnp.exp(scores - fresh[None, :]), axis=0)
        top = fresh
    global_top = lax.pmax(top, "row")
    summed = lax.psum(summed * jnp.exp(top - global_top), "row")
    top = global_top
    return top + jnp.log(summed)


def per_device(particles, log_weights, targets):
    row_count = particles.shape[0]
    block_count = max(1, row_count // 512)
    block_rows = row_count // block_count
    log_count = math.log(targets.shape[0] * lax.axis_size("col"))
    col_pot = jnp.zeros((targets.shape[0],), jnp.float32)
    col_lse = col_pot
    row_pot = log_weights
    for iteration in range(ITERS):
        row_pot = row_update(particles, log_weights, targets, col_pot, block_count, block_rows)
        col_lse = col_update(particles, targets, row_pot, block_count, block_rows)
        col_pot = EPS * (-log_count - col_lse)
    particles_half = particles.astype(jnp.bfloat16)
    acc = jnp.zeros(
        (lax.axis_size("row") * (targets.shape[0] // lax.axis_size("row")), particles.shape[1]),
        jnp.float32,
    )
    for index in range(block_count):
        source = particles[index * block_rows : (index + 1) * block_rows]
        potential = row_pot[index * block_rows : (index + 1) * block_rows]
        plan = jnp.exp(
            (potential[:, None] - cost_tile(source, targets)) / EPS - col_lse[None, :]
        ).astype(jnp.bfloat16)
        source_half = particles_half[index * block_rows : (index + 1) * block_rows]
        acc = acc + lax.dot_general(
            plan, source_half, (((0,), (0,)), ((), ())), preferred_element_type=jnp.float32
        )
    return lax.psum_scatter(acc, "row", scatter_dimension=0, tiled=True)


def solution(mesh):
    placed = (P("row", None), P("row"), P("col", None))
    return jax.shard_map(
        per_device, mesh=mesh, in_specs=placed, out_specs=P(("col", "row"), None), check_vma=False
    )
```

profile of v0, /device:TPU:1, one launch (start us, length us, event | category | flops | bytes accessed | tf_op | source)
XLA Modules:
  0.0 692.4 jit_solution(18334036911586414496)
XLA Ops:
  6.5 1.2 multiply_reduce_fusion.1
  7.8 1.1 convert_element_type.10
  8.9 1.5 multiply_reduce_fusion
  10.4 4.5 fusion.5
  14.9 4.9 fusion.4
  19.8 67.5 %pmax.42 = f32[1024]{0:T(1024)S(1)} all-reduce(f32[1024]{0:T(1024)S(1)} %pad_maximum_fusion), channel_id=1, replica_groups=mesh['row'=16,'col'=32] {'col'}, use_global_device_ids=true, to_apply=%region_5.0 | all-reduce | flops 1024 | bytes 8192 | tf_op jit(solution)/shard_map/pmax | solution.py:34
  87.2 3.2 exponential_reduce_fusion.10
  90.5 56.1 %psum.42 = f32[1024]{0:T(1024)S(1)} all-reduce(f32[1024]{0:T(1024)S(1)} %maximum_multiply_fusion), channel_id=1, replica_groups=mesh['row'=16,'col'=32] {'col'}, use_global_device_ids=true, to_apply=%region_8.0 | all-reduce | flops 1024 | bytes 8192 | tf_op jit(solution)/shard_map/psum | solution.py:35
  146.6 2.3 fusion.6
  150.0 52.4 %pmax.43 = f32[1536]{0:T(1024)S(1)} all-reduce(f32[1536]{0:T(1024)S(1)} %get-tuple-element.16), channel_id=1, replica_groups=mesh['row'=16,'col'=32] {'row'}, use_global_device_ids=true, to_apply=%region_11.0 | all-reduce | flops 1536 | bytes 12288 | tf_op jit(solution)/shard_map/pmax | solution.py:50
  202.4 2.6 exponential_reduce_fusion.9
  205.0 23.7 %psum.43 = f32[1536]{0:T(1024)S(1)} all-reduce(f32[1536]{0:T(1024)S(1)} %exponential_multiply_fusion.2), channel_id=1, replica_groups=mesh['row'=16,'col'=32] {'row'}, use_global_device_ids=true, to_apply=%region_14.0 | all-reduce | flops 1536 | bytes 12288 | tf_op jit(solution)/shard_map/psum | solution.py:51
  228.8 2.4 fusion.8
  231.6 1.0 exponential_reduce_fusion.7
  232.6 0.7 exponential_reduce_fusion.6
  233.4 57.7 %pmax.44 = f32[1024]{0:T(1024)S(1)} all-reduce(f32[1024]{0:T(1024)S(1)} %pad_maximum_fusion.1), channel_id=1, replica_groups=mesh['row'=16,'col'=32] {'col'}, use_global_device_ids=true, to_apply=%region_17.0 | all-reduce | flops 1024 | bytes 8192 | tf_op jit(solution)/shard_map/pmax | solution.py:34
  291.1 56.3 %psum.44 = f32[1024]{0:T(1024)S(1)} all-reduce(f32[1024]{0:T(1024)S(1)} %maximum_multiply_fusion.1), channel_id=1, replica_groups=mesh['row'=16,'col'=32] {'col'}, use_global_device_ids=true, to_apply=%region_20.0 | all-reduce | flops 1024 | bytes 8192 | tf_op jit(solution)/shard_map/psum | solution.py:35
  347.3 2.3 fusion.10
  350.7 51.8 %pmax.45 = f32[1536]{0:T(1024)S(1)} all-reduce(f32[1536]{0:T(1024)S(1)} %get-tuple-element.14), channel_id=1, replica_groups=mesh['row'=16,'col'=32] {'row'}, use_global_device_ids=true, to_apply=%region_23.0 | all-reduce | flops 1536 | bytes 12288 | tf_op jit(solution)/shard_map/pmax | solution.py:50
  402.5 2.6 exponential_reduce_fusion.5
  405.1 24.1 %psum.45 = f32[1536]{0:T(1024)S(1)} all-reduce(f32[1536]{0:T(1024)S(1)} %exponential_multiply_fusion.1), channel_id=1, replica_groups=mesh['row'=16,'col'=32] {'row'}, use_global_device_ids=true, to_apply=%region_26.0 | all-reduce | flops 1536 | bytes 12288 | tf_op jit(solution)/shard_map/psum | solution.py:51
  429.2 2.4 fusion.12
  432.0 1.0 exponential_reduce_fusion.3
  433.8 57.4 %pmax.46 = f32[1024]{0:T(1024)S(1)} all-reduce(f32[1024]{0:T(1024)S(1)} %pad_maximum_fusion.2), channel_id=1, replica_groups=mesh['row'=16,'col'=32] {'col'}, use_global_device_ids=true, to_apply=%region_29.0 | all-reduce | flops 1024 | bytes 8192 | tf_op jit(solution)/shard_map/pmax | solution.py:34
  491.2 56.1 %psum.46 = f32[1024]{0:T(1024)S(1)} all-reduce(f32[1024]{0:T(1024)S(1)} %maximum_multiply_fusion.2), channel_id=1, replica_groups=mesh['row'=16,'col'=32] {'col'}, use_global_device_ids=true, to_apply=%region_32.0 | all-reduce | flops 1024 | bytes 8192 | tf_op jit(solution)/shard_map/psum | solution.py:35
  547.4 2.3 fusion.14
  550.1 51.8 %pmax.47 = f32[1536]{0:T(1024)S(1)} all-reduce(f32[1536]{0:T(1024)S(1)} %get-tuple-element.12), channel_id=1, replica_groups=mesh['row'=16,'col'=32] {'row'}, use_global_device_ids=true, to_apply=%region_35.0 | all-reduce | flops 1536 | bytes 12288 | tf_op jit(solution)/shard_map/pmax | solution.py:50
  602.5 1.2 copy-done.2
  604.4 24.1 %psum.47 = f32[1536]{0:T(1024)S(1)} all-reduce(f32[1536]{0:T(1024)S(1)} %exponential_multiply_fusion), channel_id=1, replica_groups=mesh['row'=16,'col'=32] {'row'}, use_global_device_ids=true, to_apply=%region_38.0 | all-reduce | flops 1536 | bytes 12288 | tf_op jit(solution)/shard_map/psum | solution.py:51
  628.5 2.7 fusion.16
  631.3 1.8 convolution_add_fusion
  633.1 52.5 %reduce-scatter.2.cloned.1.call-done = f32[96,128]{1,0:T(8,128)} async-done(((f32[1536,128]{1,0:T(8,128)}), f32[96,128]{1,0:T(8,128)}) %reduce-scatter.2.cloned.1.call-update) | async-done | bytes 49168 | tf_op jit(solution)/shard_map/reduce_scatter | solution.py:83
  (42 shorter events, 5.7 us)
Async XLA Ops:
  6.5 679.0 %reduce-scatter.2.cloned.1.call-start = ((), (), s32[]{:S(2)}) async-start(), calls=%async_computation.1 | async-start | bytes 835584 | tf_op jit(solution)/shard_map/reduce_scatter | solution.py:83
  8.9 6.0 copy-start.3
  8.9 6.0 copy-start.4
  87.2 59.4 %copy-start.5 = (f32[1024]{0:T(1024)S(1)}, f32[1024]{0:T(1024)}, u32[]{:S(2)}) copy-start(f32[1024]{0:T(1024)} %param.4) | copy-start | bytes 12292
  228.8 2.8 copy-start
  429.2 2.8 copy-start.1
  601.8 1.9 copy-start.2
Sparse Core Ops, SparseCore 0:
  633.2 52.3 reduce-scatter.1
where the time goes:
time: 694 us; the launch traced here: 692 us
  blocking collectives  579 us (83%)
  waiting for transfers between devices  52.5 us (8%)
  other arithmetic  31.5 us (5%)
  matrix products  13.9 us (2%)
  between operations  13.7 us (2%)
    pmax x3, blocking collectives, row_update(): top = lax.pmax(local_top, 'col')  183 us
    psum x3, blocking collectives, row_update(): summed = lax.psum(local_sum * jnp.exp(local_top - top), 'col')  169 us
    pmax x3, blocking collectives, col_update(): global_top = lax.pmax(top, 'row')  156 us
    psum x3, blocking collectives, col_update(): summed = lax.psum(summed * jnp.exp(top - global_top), 'row')  71.8 us
    reduce_scatter x1, waiting for transfers between devices, per_device(): return lax.psum_scatter(acc, 'row', scatter_dimension=0, tiled=True)  52.5 us
  transfers between devices with their start and end apart: 1, of which 1 were waited for; matrix products, arithmetic and copies ran while one was open for 0% of the time, Pallas kernels for 0%

commit v1 on v0

v1 whole, which is shorter than its diff:
```python
import math

import jax
import jax.numpy as jnp
from jax import lax
from jax.experimental import pallas as pl
from jax.experimental.pallas import tpu as pltpu
from jax.sharding import PartitionSpec as P

ITERS = 3
EPS = 0.01
LOG2E = math.log2(math.e)
LANES = 128
SUBS = 8
VMEM = pl.BlockSpec(memory_space=pltpu.VMEM)
HBM = pl.BlockSpec(memory_space=pltpu.HBM)


def far(x):
    return pltpu.with_memory_space_constraint(x, pltpu.HBM)


def f32(*shape):
    return jax.ShapeDtypeStruct(shape, jnp.float32)


def received(ref):
    return ref[...].reshape(ref.shape[0], ref.shape[2])


def send(out_ref, lanes, row):
    out_ref[:, :, lanes] = jnp.broadcast_to(row[None], (out_ref.shape[0], 1, row.shape[1]))


def combine(parts):
    top = jnp.max(parts, axis=0, keepdims=True)
    return top + jnp.log2(jnp.sum(jnp.exp2(parts - top), axis=0, keepdims=True))


def split(x):
    high = x.astype(jnp.bfloat16)
    low = (x - high.astype(jnp.float32)).astype(jnp.bfloat16)
    return high, low


def row_partials(score_ref, pot, out_ref, spread_ref):
    rows, width = score_ref.shape
    tiles = width // LANES
    pots = None if pot is None else jnp.broadcast_to(pot, (SUBS, width))

    def body(group, carry):
        base = pl.multiple_of(group * SUBS, SUBS)
        values = []
        for tile in range(tiles):
            value = score_ref[pl.ds(base, SUBS), tile * LANES : (tile + 1) * LANES]
            if pots is not None:
                value = value + pots[:, tile * LANES : (tile + 1) * LANES]
            values.append(value)
        top = values[0]
        for value in values[1:]:
            top = jnp.maximum(top, value)
        total = jnp.exp2(values[0] - top)
        for value in values[1:]:
            total = total + jnp.exp2(value - top)
        spread_ref[pl.ds(base, SUBS), :] = top + jnp.log2(total)
        return carry

    lax.fori_loop(0, rows // SUBS, body, 0, unroll=4)
    for block in range(rows // LANES):
        lanes = slice(block * LANES, (block + 1) * LANES)
        send(out_ref, lanes, combine(spread_ref[lanes, :].T))


def spread_rows(pot, spread_ref):
    for block in range(pot.shape[1] // LANES):
        part = pot[:, block * LANES : (block + 1) * LANES]
        spread_ref[block * LANES : (block + 1) * LANES, :] = jnp.broadcast_to(part, (LANES, LANES)).T


def col_stats(score_ref, spread_ref, tile, chunk=16):
    rows = score_ref.shape[0]
    lanes = slice(tile * LANES, (tile + 1) * LANES)

    def body(step, carry):
        old_top, old_total = carry
        values = []
        for index in range(chunk):
            base = pl.multiple_of(step * (chunk * SUBS), chunk * SUBS) + index * SUBS
            values.append(score_ref[pl.ds(base, SUBS), lanes] + spread_ref[pl.ds(base, SUBS), :])
        top = old_top
        for value in values:
            top = jnp.maximum(top, value)
        total = old_total * jnp.exp2(old_top - top)
        for value in values:
            total = total + jnp.exp2(value - top)
        return top, total

    start = (jnp.full((SUBS, LANES), -1e30, jnp.float32), jnp.zeros((SUBS, LANES), jnp.float32))
    return lax.fori_loop(0, rows // (chunk * SUBS), body, start, unroll=2)


def lane_sums(ref, out_ref, scale):
    for block in range(ref.shape[0] // LANES):
        part = ref[block * LANES : (block + 1) * LANES, :]
        out_ref[:, block * LANES : (block + 1) * LANES] = (
            jnp.sum((part * part).T, axis=0, keepdims=True) * scale
        )


def first_kernel(
    place_ref, particles_hbm, weights_hbm, targets_hbm,
    score_ref, out_ref, source_sq_ref, weights_ref, mine_ref, mine_sq_ref,
    particles_ref, targets_ref, right_ref, points_sq_ref, spread_ref, sems,
):
    size = particles_ref.shape[1]
    scale = LOG2E / (EPS * size)
    rows = particles_ref.shape[0]
    copies = [
        pltpu.make_async_copy(targets_hbm, targets_ref, sems.at[0]),
        pltpu.make_async_copy(particles_hbm, particles_ref, sems.at[1]),
        pltpu.make_async_copy(weights_hbm, weights_ref, sems.at[2]),
    ]
    for copy in copies:
        copy.start()
    copies[0].wait()
    high, low = split(targets_ref[...])
    right_ref[...] = jnp.concatenate([high, low, high, low], axis=1)
    lane_sums(targets_ref, points_sq_ref, scale)
    count = mine_ref.shape[0]
    mine = targets_ref[pl.ds(pl.multiple_of(place_ref[0] * count, SUBS), count), :]
    high, low = split(mine * (2.0 * scale))
    mine_ref[...] = jnp.concatenate([high, high, low, low], axis=1)
    mine_sq_ref[...] = jnp.broadcast_to(jnp.sum(mine * mine, axis=1, keepdims=True) * scale, mine_sq_ref.shape)
    copies[1].wait()
    lane_sums(particles_ref, source_sq_ref, scale)
    points_sq = points_sq_ref[...]
    step = 256

    def body(index, carry):
        base = pl.multiple_of(index * step, step)
        source = particles_ref[pl.ds(base, step), :]
        source_sq = jnp.sum(source * source, axis=1, keepdims=True) * scale
        high, low = split(source * (2.0 * scale))
        left = jnp.concatenate([high, high, low, low], axis=1)
        cross = lax.dot_general(
            left, right_ref[...], (((1,), (1,)), ((), ())), preferred_element_type=jnp.float32
        )
        score_ref[pl.ds(base, step), :] = cross - source_sq - points_sq
        return carry

    lax.fori_loop(0, rows // step, body, 0)
    row_partials(score_ref, None, out_ref, spread_ref)
    copies[2].wait()


def row_kernel(log_count, score_ref, parts_ref, out_ref, spread_ref):
    col_pot = -log_count - combine(received(parts_ref))
    row_partials(score_ref, col_pot, out_ref, spread_ref)


def col_kernel(score_ref, parts_ref, weights_ref, out_ref, spread_ref):
    row_pot = weights_ref[...] * LOG2E - combine(received(parts_ref))
    spread_rows(row_pot, spread_ref)
    for tile in range(score_ref.shape[1] // LANES):
        top, total = col_stats(score_ref, spread_ref, tile)
        send(out_ref, slice(tile * LANES, (tile + 1) * LANES), combine(top + jnp.log2(total)))


def pot_kernel(parts_ref, weights_ref, source_sq_ref, out_ref):
    pot = weights_ref[...] * LOG2E - combine(received(parts_ref)) - source_sq_ref[...]
    send(out_ref, slice(0, pot.shape[1]), pot)


def cross_kernel(particles_ref, mine_ref, mine_sq_ref, cross_ref, half_ref):
    blocks, _, rows = cross_ref.shape
    for block in range(blocks):
        high, low = split(particles_ref[block * rows : (block + 1) * rows, :])
        half_ref[block] = high
        right = jnp.concatenate([high, low, high, low], axis=1)
        cross = lax.dot_general(
            mine_ref[...], right, (((1,), (1,)), ((), ())), preferred_element_type=jnp.float32
        )
        cross_ref[block] = cross - mine_sq_ref[:, :1]


def last_kernel(cross_hbm, pots_ref, half_hbm, out_ref, cross_ref, half_ref, plan_ref, sems):
    blocks, width, rows = cross_ref.shape
    tiles = rows // LANES

    def copy(which, block):
        source, target = ((cross_hbm, cross_ref), (half_hbm, half_ref))[which]
        return pltpu.make_async_copy(source.at[block], target.at[block], sems.at[which, block])

    for which in range(2):
        for block in range(blocks):
            copy(which, block).start()

    def largest(block, tops):
        copy(0, block).wait()
        pots = jnp.broadcast_to(pots_ref[block], (SUBS, rows))
        news = []
        for group in range(width // SUBS):
            top = tops[group]
            for tile in range(tiles):
                lanes = slice(tile * LANES, (tile + 1) * LANES)
                top = jnp.maximum(top, cross_ref[block, group * SUBS : (group + 1) * SUBS, lanes] + pots[:, lanes])
            news.append(top)
        return tuple(news)

    start = tuple(jnp.full((SUBS, LANES), -1e30, jnp.float32) for _ in range(width // SUBS))
    tops = lax.fori_loop(0, blocks, largest, start)
    tops = [jnp.broadcast_to(jnp.max(top, axis=1, keepdims=True), (SUBS, LANES)) for top in tops]

    def fill(block, carry):
        totals, acc = carry
        pots = jnp.broadcast_to(pots_ref[block], (SUBS, rows))
        news = []
        for group in range(0, width // SUBS, 2):
            pair = []
            for index in (group, group + 1):
                values = []
                total = totals[index]
                for tile in range(tiles):
                    lanes = slice(tile * LANES, (tile + 1) * LANES)
                    value = jnp.exp2(
                        cross_ref[block, index * SUBS : (index + 1) * SUBS, lanes] + pots[:, lanes] - tops[index]
                    )
                    values.append(value)
                    total = total + value
                news.append(total)
                pair.append(values)
            for tile in range(tiles):
                plan_ref[group * SUBS : (group + 2) * SUBS, tile * LANES : (tile + 1) * LANES] = jnp.concatenate(
                    [pair[0][tile], pair[1][tile]], axis=0
                ).astype(jnp.bfloat16)
        copy(1, block).wait()
        acc = acc + jnp.dot(plan_ref[...], half_ref[block], preferred_element_type=jnp.float32)
        return tuple(news), acc

    zeros = tuple(jnp.zeros((SUBS, LANES), jnp.float32) for _ in range(width // SUBS))
    totals, acc = lax.fori_loop(0, blocks, fill, (zeros, jnp.zeros(out_ref.shape, jnp.float32)))
    total = jnp.concatenate([jnp.sum(total, axis=1, keepdims=True) for total in totals], axis=0)
    out_ref[...] = acc / total


def exchange(sent, axis):
    return lax.all_to_all(sent, axis, 0, 0, tiled=True)


def per_device(particles, log_weights, targets):
    rows, size = particles.shape
    width = targets.shape[0]
    row_axes, col_axes = ("y", "core"), ("z", "x")
    row_count = lax.axis_size(row_axes)
    log_count = math.log2(width * lax.axis_size(col_axes))
    params = pltpu.CompilerParams(vmem_limit_bytes=12 * 1024 * 1024)
    spread = pltpu.VMEM((rows, LANES), jnp.float32)
    kept = pltpu.VMEM((rows, width), jnp.float32)
    block = width // row_count
    place = lax.axis_index(row_axes).astype(jnp.int32).reshape(1)
    every = lax.all_gather(particles, row_axes, tiled=True)
    to_cols = f32(lax.axis_size(col_axes), 1, rows)
    to_rows = f32(row_count, 1, width)

    score, local, source_sq, weights, mine, mine_sq = pl.pallas_call(
        first_kernel,
        out_shape=(
            kept, to_cols, f32(1, rows), f32(1, rows),
            jax.ShapeDtypeStruct((block, 4 * size), jnp.bfloat16), f32(block, LANES),
        ),
        in_specs=[pl.BlockSpec(memory_space=pltpu.SMEM)] + [HBM] * 3,
        out_specs=(VMEM,) * 6,
        scratch_shapes=[
            pltpu.VMEM((rows, size), jnp.float32),
            pltpu.VMEM((width, size), jnp.float32),
            pltpu.VMEM((width, 4 * size), jnp.bfloat16),
            pltpu.VMEM((1, width), jnp.float32),
            spread,
            pltpu.SemaphoreType.DMA((3,)),
        ],
        compiler_params=params,
    )(place, far(particles), far(log_weights.reshape(1, rows)), far(targets))
    for iteration in range(ITERS):
        if iteration:
            local = pl.pallas_call(
                lambda *refs: row_kernel(log_count, *refs),
                name="row_kernel",
                out_shape=to_cols,
                in_specs=[VMEM] * 2,
                out_specs=VMEM,
                scratch_shapes=[spread],
                compiler_params=params,
            )(score, parts)
        if iteration == ITERS - 1:
            local, every = lax.optimization_barrier((local, every))
        parts = exchange(local, col_axes)
        if iteration == ITERS - 1:
            break
        local = pl.pallas_call(
            col_kernel,
            out_shape=to_rows,
            in_specs=[VMEM] * 3,
            out_specs=VMEM,
            scratch_shapes=[spread],
            compiler_params=params,
        )(score, parts, weights)
        parts = exchange(local, row_axes)
    step = 2
    cross, half = pl.pallas_call(
        cross_kernel,
        grid=(row_count // step,),
        out_shape=(
            pltpu.HBM((row_count, block, rows), jnp.float32),
            pltpu.HBM((row_count, rows, size), jnp.bfloat16),
        ),
        in_specs=[
            pl.BlockSpec((step * rows, size), lambda index: (index, 0)),
            pl.BlockSpec((block, 4 * size), lambda index: (0, 0)),
            pl.BlockSpec((block, LANES), lambda index: (0, 0)),
        ],
        out_specs=(
            pl.BlockSpec((step, block, rows), lambda index: (index, 0, 0)),
            pl.BlockSpec((step, rows, size), lambda index: (index, 0, 0)),
        ),
        compiler_params=pltpu.CompilerParams(vmem_limit_bytes=16 * 1024 * 1024),
        cost_estimate=pl.CostEstimate(
            flops=8 * row_count * rows * block * size,
            bytes_accessed=row_count * rows * (6 * size + 4 * block),
            transcendentals=0,
        ),
    )(far(every), mine, mine_sq)
    parts, cross, half = lax.optimization_barrier((parts, cross, half))
    pots = pl.pallas_call(
        pot_kernel,
        out_shape=f32(row_count, 1, rows),
        in_specs=[VMEM] * 3,
        out_specs=VMEM,
        compiler_params=params,
    )(parts, weights, source_sq)
    pots = exchange(pots, row_axes)
    return pl.pallas_call(
        last_kernel,
        out_shape=f32(block, size),
        in_specs=[HBM, VMEM, HBM],
        out_specs=VMEM,
        scratch_shapes=[
            pltpu.VMEM((row_count, block, rows), jnp.float32),
            pltpu.VMEM((row_count, rows, size), jnp.bfloat16),
            pltpu.VMEM((block, rows), jnp.bfloat16),
            pltpu.SemaphoreType.DMA((2, row_count)),
        ],
        compiler_params=pltpu.CompilerParams(vmem_limit_bytes=16 * 1024 * 1024),
    )(far(cross), pots, far(half))


def solution(mesh):
    shape = dict(mesh.shape)
    row, col = shape["row"], shape["col"]
    devices = mesh.devices.reshape(row // 2, 2, col // 4, 4)
    parts = jax.sharding.Mesh(devices, ("y", "core", "z", "x"))
    rows, cols = ("y", "core"), ("z", "x")
    return jax.shard_map(
        per_device,
        mesh=parts,
        in_specs=(P(rows, None), P(rows), P(cols, None)),
        out_specs=P(cols + rows, None),
        check_vma=False,
    )
```

time: 694 us -> 135 us (0.19)
  blocking collectives: 579 us -> 77.3 us
  waiting for transfers between devices: 52.5 us -> 0.71 us
  Pallas kernels: 0 us -> 38.8 us
  other arithmetic: 31.5 us -> 0 us
  matrix products: 13.9 us -> 0 us
    pmax x6 -> x0, blocking collectives: 338 us -> none  [the longest x3 183 us: row_update(): top = lax.pmax(local_top, 'col')]
    psum x6 -> x0, blocking collectives: 240 us -> none  [the longest x3 169 us: row_update(): summed = lax.psum(local_sum * jnp.exp(local_top - top), 'col')]
    all_to_all x0 -> x5, blocking collectives: none -> 77.3 us  [exchange(): return lax.all_to_all(sent, axis, 0, 0, tiled=True)]
    reduce_scatter x1 -> x0, waiting for transfers between devices: 52.5 us -> none  [per_device(): return lax.psum_scatter(acc, 'row', scatter_dimension=0, tiled=True)]
    pallas_call x0 -> x8, Pallas kernels: none -> 38.8 us  [the longest x1 11.1 us: per_device(): pl.pallas_call(cross_kernel, grid=(row_count // step,), out_shape=(pltpu....]
    reduce_sum x13 -> x0, other arithmetic: 17.4 us -> none  [the longest x6 7.93 us: col_update(): jnp.sum(jnp.exp(scores - fresh[None, :]), axis=0)]
    dot_general x4 -> x0, matrix products: 13.9 us -> none  [the longest x2 9.35 us: cost_tile(): jnp.dot(source, points.T, precision=lax.Precision.HIGHEST, preferred_elem...]
    reduce_max x8 -> x0, other arithmetic: 12.8 us -> none  [the longest x6 7.98 us: col_update(): fresh = jnp.maximum(top, jnp.max(scores, axis=0))]
  transfers between devices with their start and end apart: 1 -> 2, of which waited for: 1 -> 0; matrix products, arithmetic and copies ran while one was open for 0% -> 0% of each run, Pallas kernels for 0% -> 23%
where the time goes in v1:
time: 135 us; the launch traced here: 134 us
  blocking collectives  77.3 us (57%)
  Pallas kernels  38.8 us (29%)
  between operations  13.5 us (10%)
  starting transfers between devices  3.85 us (3%)
    all_to_all x5, blocking collectives, exchange(): return lax.all_to_all(sent, axis, 0, 0, tiled=True)  77.3 us
    pallas_call x1, Pallas kernels, per_device(): pl.pallas_call(cross_kernel, grid=(row_count // step,), out_shape=(pltpu....  11.1 us
    pallas_call x1, Pallas kernels, per_device(): pl.pallas_call(last_kernel, out_shape=f32(block, size), in_specs=[HBM, VM...  8.32 us
    pallas_call x2, Pallas kernels, per_device(): pl.pallas_call(col_kernel, out_shape=to_rows, in_specs=[VMEM] * 3, out_sp...  7.63 us
    pallas_call x1, Pallas kernels, per_device(): pl.pallas_call(first_kernel, out_shape=(kept, to_cols, f32(1, rows), f32(...  6.43 us
    pallas_call x2, Pallas kernels, per_device(): pl.pallas_call(lambda *refs: row_kernel(log_count, *refs), name='row_kern...  5.25 us
    all_to_all x1, starting transfers between devices, exchange(): return lax.all_to_all(sent, axis, 0, 0, tiled=True)  3.84 us
  transfers between devices with their start and end apart: 2, of which 0 were waited for; matrix products, arithmetic and copies ran while one was open for 0% of the time, Pallas kernels for 23%

profile of v1, /device:TPU:1, one launch (start us, length us, event | category | flops | bytes accessed | tf_op | source)
XLA Modules:
  0.0 134.2 jit_solution(18278960028367516742)
XLA Ops:
  6.5 0.0 all-gather.2.cloned.1.call-start
  6.5 0.7 all-gather.2.cloned.1.call-update
  7.3 6.4 %shard_map.37 = (f32[1024,1536]{1,0:T(8,128)S(1)}, f32[32,1,1024]{2,1,0:T(1,128)S(1)}, f32[1,1024]{1,0:T(1,128)S(1)}, f32[1,1024]{1,0:T(1,128)S(1)}, bf16[96,512]{1,0:T(8,128)(2,1)S(1)}, /*index=5*/f32[96,128]{1,0:T(8,128)S(1)}) custom-call(s32[1]{0:T(128)} %bitcast.place_ref, f32[1024,128]{1,0:T(8,128)} %particles_hbm.1, f32[1,1024]{1,0:T(1,128)} %bitcast.2, ...), custom_call_target="tpu_custom_call" | custom-call | tf_op jit(solution)/shard_map/pallas_call | solution.py:265
  13.7 22.9 %all_to_all.30.parts_ref = f32[32,1,1024]{2,1,0:T(1,128)S(1)} all-to-all(f32[32,1,1024]{2,1,0:T(1,128)S(1)} %get-tuple-element.19), channel_id=1, replica_groups=mesh['y'=8,'core'=2,'z'=8,'x'=4] {'z','x'}, dimensions={0} | all-to-all | bytes 262144 | tf_op jit(solution)/shard_map/all_to_all | solution.py:247
  36.6 3.8 %shard_map.38 = f32[16,1,1536]{2,1,0:T(1,128)S(1)} custom-call(f32[1024,1536]{1,0:T(8,128)S(1)} %get-tuple-element.18.score_ref.refs_0_, f32[32,1,1024]{2,1,0:T(1,128)S(1)} %all_to_all.30.parts_ref, f32[1,1024]{1,0:T(1,128)S(1)} %get-tuple-element.20.weights_ref), custom_call_target="tpu_custom_call" | custom-call | tf_op jit(solution)/shard_map/pallas_call | solution.py:299
  40.4 18.6 %all_to_all.31.refs_1_ = f32[16,1,1536]{2,1,0:T(1,128)S(1)} all-to-all(f32[16,1,1536]{2,1,0:T(1,128)S(1)} %shard_map.38), channel_id=1, replica_groups=mesh['y'=8,'core'=2,'z'=8,'x'=4] {'y','core'}, dimensions={0} | all-to-all | bytes 196608 | tf_op jit(solution)/shard_map/all_to_all | solution.py:247
  59.0 2.3 %row_kernel.2 = f32[32,1,1024]{2,1,0:T(1,128)S(1)} custom-call(f32[1024,1536]{1,0:T(8,128)S(1)} %get-tuple-element.18.score_ref.refs_0_, f32[16,1,1536]{2,1,0:T(1,128)S(1)} %all_to_all.31.refs_1_), custom_call_target="tpu_custom_call" | custom-call | tf_op jit(solution)/shard_map/row_kernel/pallas_call | solution.py:285
  61.3 13.0 %all_to_all.32.parts_ref = f32[32,1,1024]{2,1,0:T(1,128)S(1)} all-to-all(f32[32,1,1024]{2,1,0:T(1,128)S(1)} %row_kernel.2), channel_id=1, replica_groups=mesh['y'=8,'core'=2,'z'=8,'x'=4] {'z','x'}, dimensions={0} | all-to-all | bytes 262144 | tf_op jit(solution)/shard_map/all_to_all | solution.py:247
  74.3 3.8 %shard_map.39 = f32[16,1,1536]{2,1,0:T(1,128)S(1)} custom-call(f32[1024,1536]{1,0:T(8,128)S(1)} %get-tuple-element.18.score_ref.refs_0_, f32[32,1,1024]{2,1,0:T(1,128)S(1)} %all_to_all.32.parts_ref, f32[1,1024]{1,0:T(1,128)S(1)} %get-tuple-element.20.weights_ref), custom_call_target="tpu_custom_call" | custom-call | tf_op jit(solution)/shard_map/pallas_call | solution.py:299
  78.2 12.3 %all_to_all.33.refs_1_ = f32[16,1,1536]{2,1,0:T(1,128)S(1)} all-to-all(f32[16,1,1536]{2,1,0:T(1,128)S(1)} %shard_map.39), channel_id=1, replica_groups=mesh['y'=8,'core'=2,'z'=8,'x'=4] {'y','core'}, dimensions={0} | all-to-all | bytes 196608 | tf_op jit(solution)/shard_map/all_to_all | solution.py:247
  90.5 2.9 %row_kernel.3 = f32[32,1,1024]{2,1,0:T(1,128)} custom-call(f32[1024,1536]{1,0:T(8,128)S(1)} %get-tuple-element.18.score_ref.refs_0_, f32[16,1,1536]{2,1,0:T(1,128)S(1)} %all_to_all.33.refs_1_), custom_call_target="tpu_custom_call" | custom-call | tf_op jit(solution)/shard_map/row_kernel/pallas_call | solution.py:285
  93.4 0.0 all-gather.2.cloned.1.call-done.particles_ref
  93.4 3.8 %all-to-all-start.4 = ((f32[32,1,1024]{2,1,0:T(1,128)}), f32[32,1,1024]{2,1,0:T(1,128)S(1)}, u32[]{:S(2)}, u32[]{:S(2)}) async-start(f32[32,1,1024]{2,1,0:T(1,128)} %row_kernel.3), calls=%async_computation.4 | async-start | bytes 262144 | tf_op jit(solution)/shard_map/all_to_all | solution.py:247
  97.3 11.1 %shard_map.40 = (f32[16,96,1024]{2,1,0:T(8,128)}, bf16[16,1024,128]{2,1,0:T(8,128)(2,1)}) custom-call(f32[16384,128]{1,0:T(8,128)} %all-gather.2.cloned.1.call-done.particles_ref, bf16[96,512]{1,0:T(8,128)(2,1)S(1)} %get-tuple-element.23.mine_ref, f32[96,128]{1,0:T(8,128)S(1)} %get-tuple-element.24.mine_sq_ref), custom_call_target="tpu_custom_call" | custom-call | flops 1610612736 | bytes 18874368 | tf_op jit(solution)/shard_map/pallas_call | solution.py:309
  108.4 0.0 all-to-all-done.4.parts_ref
  108.4 0.1 shard_map.41
  108.5 10.5 %all_to_all.34.pots_ref = f32[16,1,1024]{2,1,0:T(1,128)S(1)} all-to-all(f32[16,1,1024]{2,1,0:T(1,128)S(1)} %shard_map.41), channel_id=1, replica_groups=mesh['y'=8,'core'=2,'z'=8,'x'=4] {'y','core'}, dimensions={0} | all-to-all | bytes 131072 | tf_op jit(solution)/shard_map/all_to_all | solution.py:247
  119.0 8.3 %shard_map.42 = f32[96,128]{1,0:T(8,128)} custom-call(f32[16,96,1024]{2,1,0:T(8,128)} %get-tuple-element.27.cross_hbm, f32[16,1,1024]{2,1,0:T(1,128)S(1)} %all_to_all.34.pots_ref, bf16[16,1024,128]{2,1,0:T(8,128)(2,1)} %get-tuple-element.30.half_hbm), custom_call_target="tpu_custom_call" | custom-call | tf_op jit(solution)/shard_map/pallas_call | solution.py:341
Async XLA Ops:
  6.5 86.9 %all-gather.2.cloned.1.call-start = ((), (), s32[]{:S(2)}) async-start(), calls=%async_computation.6 | async-start | bytes 8912896 | tf_op jit(solution)/shard_map/all_gather | solution.py:261
  93.4 15.0 %all-to-all-start.4 = ((f32[32,1,1024]{2,1,0:T(1,128)}), f32[32,1,1024]{2,1,0:T(1,128)S(1)}, u32[]{:S(2)}, u32[]{:S(2)}) async-start(f32[32,1,1024]{2,1,0:T(1,128)} %row_kernel.3), calls=%async_computation.4 | async-start | bytes 262144 | tf_op jit(solution)/shard_map/all_to_all | solution.py:247
Sparse Core Ops, SparseCore 0:
  9.5 66.2 all-gather.1

commit v2 on v0

v2 whole, which is shorter than its diff:
```python
import math

import jax
import jax.numpy as jnp
from jax import lax
from jax.experimental import pallas as pl
from jax.experimental.pallas import tpu as pltpu
from jax.sharding import PartitionSpec as P

ITERS = 3
EPS = 0.01
LOG2E = math.log2(math.e)
LANES = 128
SUBS = 8
CHUNK = 128
STATS = 8
LOWEST = -1e30
VMEM = pl.BlockSpec(memory_space=pltpu.VMEM)
HBM = pl.BlockSpec(memory_space=pltpu.HBM)


def far(x):
    return pltpu.with_memory_space_constraint(x, pltpu.HBM)


def f32(*shape):
    return jax.ShapeDtypeStruct(shape, jnp.float32)


def lanes_of(tile):
    return slice(tile * LANES, (tile + 1) * LANES)


def received(ref):
    return ref[...].reshape(ref.shape[0], ref.shape[2])


def send(out_ref, lanes, row):
    out_ref[:, :, lanes] = jnp.broadcast_to(row[None], (out_ref.shape[0], 1, row.shape[1]))


def combine(parts):
    top = jnp.max(parts, axis=0, keepdims=True)
    return top + jnp.log2(jnp.sum(jnp.exp2(parts - top), axis=0, keepdims=True))


def split(x):
    high = x.astype(jnp.bfloat16)
    low = (x - high.astype(jnp.float32)).astype(jnp.bfloat16)
    return high, low


def tree(op, values):
    while len(values) > 1:
        values = [op(*values[i : i + 2]) if i + 1 < len(values) else values[i] for i in range(0, len(values), 2)]
    return values[0]


def lane_lse(values):
    top = tree(jnp.maximum, values)
    return top + jnp.log2(tree(jnp.add, [jnp.exp2(value - top) for value in values]))


def row_group(score_ref, base, pots, spread_ref):
    values = []
    for tile in range(score_ref.shape[1] // LANES):
        value = score_ref[pl.ds(base, SUBS), lanes_of(tile)]
        values.append(value if pots is None else value + pots[:, lanes_of(tile)])
    spread_ref[pl.ds(base, SUBS), :] = lane_lse(values)


def send_rows(spread_ref, out_ref):
    for block in range(spread_ref.shape[0] // LANES):
        send(out_ref, lanes_of(block), combine(spread_ref[lanes_of(block), :].T))


def spread_rows(pot, spread_ref):
    for block in range(pot.shape[1] // LANES):
        spread_ref[lanes_of(block), :] = jnp.broadcast_to(pot[:, lanes_of(block)], (LANES, LANES)).T


def first_kernel(
    particles_hbm, weights_hbm, targets_hbm,
    score_ref, out_ref, weights_ref, half_ref,
    particles_ref, targets_ref, right_ref, points_sq_ref, spread_ref, sems,
):
    rows, size = particles_ref.shape
    scale = LOG2E / (EPS * size)
    copies = [
        pltpu.make_async_copy(targets_hbm, targets_ref, sems.at[0]),
        pltpu.make_async_copy(particles_hbm, particles_ref, sems.at[1]),
        pltpu.make_async_copy(weights_hbm, weights_ref, sems.at[2]),
    ]
    for copy in copies:
        copy.start()
    copies[0].wait()
    for tile in range(targets_ref.shape[0] // LANES):
        lanes = lanes_of(tile)
        part = targets_ref[lanes, :].T
        points_sq_ref[:, lanes] = jnp.sum(part * part, axis=0, keepdims=True) * scale
        high, low = split(part)
        for index, half in enumerate((high, low, high, low)):
            right_ref[index * size : (index + 1) * size, lanes] = half
    copies[1].wait()
    copies[2].wait()
    points_sq = points_sq_ref[...]
    step = 256

    def scores(index):
        part = slice(index * step, (index + 1) * step)
        source = particles_ref[part, :]
        source_sq = jnp.sum(source * source, axis=1, keepdims=True) * scale
        high, low = split(source * (2.0 * scale))
        left = jnp.concatenate([high, high, low, low], axis=1)
        cross = jnp.dot(left, right_ref[...], preferred_element_type=jnp.float32)
        score_ref[part, :] = cross - source_sq - points_sq
        half_ref[:, part] = source.T.astype(jnp.bfloat16)

    def partials(index):
        for group in range(step // SUBS):
            row_group(score_ref, index * step + group * SUBS, None, spread_ref)

    for index in range(rows // step):
        scores(index)
        if index:
            partials(index - 1)
    partials(rows // step - 1)
    send_rows(spread_ref, out_ref)


def row_kernel(log_count, score_ref, parts_ref, out_ref, spread_ref):
    col_pot = -log_count - combine(received(parts_ref))
    pots = jnp.broadcast_to(col_pot, (SUBS, col_pot.shape[1]))

    def body(group, carry):
        row_group(score_ref, pl.multiple_of(group * SUBS, SUBS), pots, spread_ref)
        return carry

    lax.fori_loop(0, score_ref.shape[0] // SUBS, body, 0, unroll=8)
    send_rows(spread_ref, out_ref)


def col_chunk(score_ref, spread_ref, step):
    base = pl.multiple_of(step * CHUNK, CHUNK)
    pots = [spread_ref[pl.ds(base + index * SUBS, SUBS), :] for index in range(CHUNK // SUBS)]
    for tile in range(score_ref.shape[1] // LANES):
        yield tile, [
            score_ref[pl.ds(base + index * SUBS, SUBS), lanes_of(tile)] + pot for index, pot in enumerate(pots)
        ]


def col_kernel(score_ref, parts_ref, weights_ref, out_ref, spread_ref, chunk_ref):
    rows, width = score_ref.shape
    row_pot = weights_ref[...] * LOG2E - combine(received(parts_ref))
    spread_rows(row_pot, spread_ref)

    def body(step, carry):
        for tile, values in col_chunk(score_ref, spread_ref, step):
            chunk_ref[pl.ds(pl.multiple_of(step * SUBS, SUBS), SUBS), lanes_of(tile)] = lane_lse(values)
        return carry

    lax.fori_loop(0, rows // CHUNK, body, 0)
    send(out_ref, slice(0, width), combine(chunk_ref[...]))


def last_kernel(score_ref, parts_ref, weights_ref, half_ref, out_ref, spread_ref, plan_ref):
    rows, width = score_ref.shape
    tiles = width // LANES
    row_pot = weights_ref[...] * LOG2E - combine(received(parts_ref))
    spread_rows(row_pot, spread_ref)

    def largest(step, tops):
        news = []
        for tile, values in col_chunk(score_ref, spread_ref, step):
            news.append(jnp.maximum(tops[tile], tree(jnp.maximum, values)))
        return tuple(news)

    tops = lax.fori_loop(
        0, rows // CHUNK, largest, tuple(jnp.full((SUBS, LANES), LOWEST, jnp.float32) for _ in range(tiles))
    )
    top = jnp.concatenate([jnp.max(top, axis=0, keepdims=True) for top in tops], axis=1)
    every = jnp.broadcast_to(top, (SUBS, width))

    def fill(step, totals):
        news = []
        for tile, values in col_chunk(score_ref, spread_ref, step):
            values = [jnp.exp2(value - every[:, lanes_of(tile)]) for value in values]
            news.append(totals[tile] + tree(jnp.add, values))
            for index in range(0, len(values), 2):
                base = pl.multiple_of(step * CHUNK, CHUNK) + index * SUBS
                plan_ref[pl.ds(base, 2 * SUBS), lanes_of(tile)] = jnp.concatenate(
                    values[index : index + 2], axis=0
                ).astype(jnp.bfloat16)
        return tuple(news)

    totals = lax.fori_loop(
        0, rows // CHUNK, fill, tuple(jnp.zeros((SUBS, LANES), jnp.float32) for _ in range(tiles))
    )
    total = jnp.concatenate([jnp.sum(total, axis=0, keepdims=True) for total in totals], axis=1)
    sums = jnp.dot(half_ref[...], plan_ref[...], preferred_element_type=jnp.float32)
    sums = jnp.concatenate([sums[:, lanes_of(tile)].T for tile in range(tiles)], axis=0)
    cores, chips, block = out_ref.shape[0], out_ref.shape[1], out_ref.shape[2] - STATS
    rest = jnp.zeros((1, LANES - block), jnp.float32)
    for chip in range(chips):
        for core in range(cores):
            start = (chip * cores + core) * block
            out_ref[core, chip, :block, :] = sums[start : start + block]
            for index, row in enumerate((top, total)):
                out_ref[core, chip, block + index : block + index + 1, :] = jnp.concatenate(
                    [row[:, start : start + block], rest], axis=1
                )
            out_ref[core, chip, block + 2 :, :] = jnp.zeros((STATS - 2, LANES), jnp.float32)


def exchange(sent, axis):
    return lax.all_to_all(sent, axis, 0, 0, tiled=True)


def merge(blocks, block):
    sums = blocks[..., :block, :]
    tops = blocks[..., block, :block]
    totals = blocks[..., block + 1, :block]
    top = jnp.max(tops, axis=0)
    weight = jnp.exp2(tops - top[None])
    return jnp.sum(sums * weight[..., None], axis=0), top, jnp.sum(totals * weight, axis=0)


def pack(sums, tops, totals):
    stats = jnp.stack([tops, totals], axis=-2)
    pad = [(0, STATS - 2), (0, LANES - tops.shape[-1])]
    stats = jnp.pad(stats, [(0, 0)] * (stats.ndim - 2) + pad)
    return jnp.concatenate([sums, stats], axis=-2)


def per_device(particles, log_weights, targets):
    rows, size = particles.shape
    width = targets.shape[0]
    row_axes, col_axes = ("y", "core"), ("z", "x")
    chips, cores = lax.axis_size("y"), lax.axis_size("core")
    block = width // (chips * cores)
    log_count = math.log2(width * lax.axis_size(col_axes))
    params = pltpu.CompilerParams(vmem_limit_bytes=12 * 1024 * 1024)
    spread = pltpu.VMEM((rows, LANES), jnp.float32)
    to_cols = f32(lax.axis_size(col_axes), 1, rows)
    to_rows = f32(chips * cores, 1, width)

    score, local, weights, half = pl.pallas_call(
        first_kernel,
        out_shape=(f32(rows, width), to_cols, f32(1, rows), jax.ShapeDtypeStruct((size, rows), jnp.bfloat16)),
        in_specs=[HBM] * 3,
        out_specs=(VMEM,) * 4,
        scratch_shapes=[
            pltpu.VMEM((rows, size), jnp.float32),
            pltpu.VMEM((width, size), jnp.float32),
            pltpu.VMEM((4 * size, width), jnp.bfloat16),
            pltpu.VMEM((1, width), jnp.float32),
            spread,
            pltpu.SemaphoreType.DMA((3,)),
        ],
        compiler_params=params,
    )(far(particles), far(log_weights.reshape(1, rows)), far(targets))
    for iteration in range(ITERS):
        if iteration:
            local = pl.pallas_call(
                lambda *refs: row_kernel(log_count, *refs),
                name="row_kernel",
                out_shape=to_cols,
                in_specs=[VMEM] * 2,
                out_specs=VMEM,
                scratch_shapes=[spread],
                compiler_params=params,
            )(score, parts)
        parts = exchange(local, col_axes)
        if iteration == ITERS - 1:
            break
        local = pl.pallas_call(
            col_kernel,
            out_shape=to_rows,
            in_specs=[VMEM] * 3,
            out_specs=VMEM,
            scratch_shapes=[spread, pltpu.VMEM((rows // CHUNK * SUBS, width), jnp.float32)],
            compiler_params=params,
        )(score, parts, weights)
        parts = exchange(local, row_axes)
    blocks = pl.pallas_call(
        last_kernel,
        out_shape=f32(cores, chips, block + STATS, size),
        in_specs=[VMEM] * 4,
        out_specs=VMEM,
        scratch_shapes=[spread, pltpu.VMEM((rows, width), jnp.bfloat16)],
        compiler_params=params,
    )(score, parts, weights, half)
    blocks = exchange(blocks, "core")
    blocks = exchange(pack(*merge(blocks, block)), "y")
    sums, _, total = merge(blocks, block)
    return sums / total[:, None]


def solution(mesh):
    shape = dict(mesh.shape)
    row, col = shape["row"], shape["col"]
    devices = mesh.devices.reshape(row // 2, 2, col // 4, 4)
    parts = jax.sharding.Mesh(devices, ("y", "core", "z", "x"))
    rows, cols = ("y", "core"), ("z", "x")
    return jax.shard_map(
        per_device,
        mesh=parts,
        in_specs=(P(rows, None), P(rows), P(cols, None)),
        out_specs=P(cols + rows, None),
        check_vma=False,
    )
```

time: 694 us -> 118 us (0.17)
  blocking collectives: 579 us -> 102 us
  waiting for transfers between devices: 52.5 us -> 0 us
  other arithmetic: 31.5 us -> 1.26 us
  Pallas kernels: 0 us -> 14.3 us
  matrix products: 13.9 us -> 0 us
  between operations: 13.7 us -> 0.08 us
    pmax x6 -> x0, blocking collectives: 338 us -> none  [the longest x3 183 us: row_update(): top = lax.pmax(local_top, 'col')]
    psum x6 -> x0, blocking collectives: 240 us -> none  [the longest x3 169 us: row_update(): summed = lax.psum(local_sum * jnp.exp(local_top - top), 'col')]
    all_to_all x0 -> x7, blocking collectives: none -> 102 us  [exchange(): return lax.all_to_all(sent, axis, 0, 0, tiled=True)]
    reduce_scatter x1 -> x0, waiting for transfers between devices: 52.5 us -> none  [per_device(): return lax.psum_scatter(acc, 'row', scatter_dimension=0, tiled=True)]
    reduce_sum x13 -> x4, other arithmetic: 17.4 us -> 0.48 us  [the longest x2 0.44 us: merge(): jnp.sum(sums * weight[..., None], axis=0)]
    pallas_call x0 -> x6, Pallas kernels: none -> 14.3 us  [the longest x1 4.31 us: per_device(): pl.pallas_call(first_kernel, out_shape=(f32(rows, width), to_cols, f32(1,...]
    dot_general x4 -> x0, matrix products: 13.9 us -> none  [the longest x2 9.35 us: cost_tile(): jnp.dot(source, points.T, precision=lax.Precision.HIGHEST, preferred_elem...]
    reduce_max x8 -> x2, other arithmetic: 12.8 us -> 0.03 us  [merge(): top = jnp.max(tops, axis=0)]
  transfers between devices with their start and end apart: 1 -> 0, of which waited for: 1 -> 0; matrix products, arithmetic and copies ran while one was open for 0% -> 0% of each run, Pallas kernels for 0% -> 0%
where the time goes in v2:
time: 118 us
  blocking collectives  102 us (86%)
  Pallas kernels  14.3 us (12%)
  other arithmetic  1.26 us (1%)
    all_to_all x7, blocking collectives, exchange(): return lax.all_to_all(sent, axis, 0, 0, tiled=True)  102 us
    pallas_call x1, Pallas kernels, per_device(): pl.pallas_call(first_kernel, out_shape=(f32(rows, width), to_cols, f32(1,...  4.31 us
    pallas_call x2, Pallas kernels, per_device(): pl.pallas_call(col_kernel, out_shape=to_rows, in_specs=[VMEM] * 3, out_sp...  3.5 us
    pallas_call x2, Pallas kernels, per_device(): pl.pallas_call(lambda *refs: row_kernel(log_count, *refs), name='row_kern...  3.45 us
    pallas_call x1, Pallas kernels, per_device(): pl.pallas_call(last_kernel, out_shape=f32(cores, chips, block + STATS, si...  2.99 us

profile of v2, /device:TPU:1, one launch (start us, length us, event | category | flops | bytes accessed | tf_op | source)
XLA Modules:
  0.0 118.0 jit_solution(1118872742727768263)
XLA Ops:
  0.0 4.3 %shard_map.37 = (f32[1024,1536]{1,0:T(8,128)S(1)}, f32[32,1,1024]{2,1,0:T(1,128)S(1)}, f32[1,1024]{1,0:T(1,128)S(1)}, bf16[128,1024]{1,0:T(8,128)(2,1)S(1)}) custom-call(f32[1024,128]{1,0:T(8,128)} %particles_hbm.1, f32[1,1024]{1,0:T(1,128)} %bitcast.19, f32[1536,128]{1,0:T(8,128)} %targets_hbm.1), custom_call_target="tpu_custom_call" | custom-call | tf_op jit(solution)/shard_map/pallas_call | solution.py:247
  4.3 22.9 %all_to_all.35.parts_ref = f32[32,1,1024]{2,1,0:T(1,128)S(1)} all-to-all(f32[32,1,1024]{2,1,0:T(1,128)S(1)} %get-tuple-element.10), channel_id=1, replica_groups=mesh['y'=8,'core'=2,'z'=8,'x'=4] {'z','x'}, dimensions={0} | all-to-all | bytes 262144 | tf_op jit(solution)/shard_map/all_to_all | solution.py:216
  27.2 1.8 %shard_map.38 = f32[16,1,1536]{2,1,0:T(1,128)S(1)} custom-call(f32[1024,1536]{1,0:T(8,128)S(1)} %get-tuple-element.9.score_ref.refs_0_, f32[32,1,1024]{2,1,0:T(1,128)S(1)} %all_to_all.35.parts_ref, f32[1,1024]{1,0:T(1,128)S(1)} %get-tuple-element.11.weights_ref), custom_call_target="tpu_custom_call" | custom-call | tf_op jit(solution)/shard_map/pallas_call | solution.py:276
  28.9 17.5 %all_to_all.36.refs_1_ = f32[16,1,1536]{2,1,0:T(1,128)S(1)} all-to-all(f32[16,1,1536]{2,1,0:T(1,128)S(1)} %shard_map.38), channel_id=1, replica_groups=mesh['y'=8,'core'=2,'z'=8,'x'=4] {'y','core'}, dimensions={0} | all-to-all | bytes 196608 | tf_op jit(solution)/shard_map/all_to_all | solution.py:216
  46.4 1.7 %row_kernel.2 = f32[32,1,1024]{2,1,0:T(1,128)S(1)} custom-call(f32[1024,1536]{1,0:T(8,128)S(1)} %get-tuple-element.9.score_ref.refs_0_, f32[16,1,1536]{2,1,0:T(1,128)S(1)} %all_to_all.36.refs_1_), custom_call_target="tpu_custom_call" | custom-call | tf_op jit(solution)/shard_map/row_kernel/pallas_call | solution.py:264
  48.1 13.0 %all_to_all.37.parts_ref = f32[32,1,1024]{2,1,0:T(1,128)S(1)} all-to-all(f32[32,1,1024]{2,1,0:T(1,128)S(1)} %row_kernel.2), channel_id=1, replica_groups=mesh['y'=8,'core'=2,'z'=8,'x'=4] {'z','x'}, dimensions={0} | all-to-all | bytes 262144 | tf_op jit(solution)/shard_map/all_to_all | solution.py:216
  61.1 1.8 %shard_map.39 = f32[16,1,1536]{2,1,0:T(1,128)S(1)} custom-call(f32[1024,1536]{1,0:T(8,128)S(1)} %get-tuple-element.9.score_ref.refs_0_, f32[32,1,1024]{2,1,0:T(1,128)S(1)} %all_to_all.37.parts_ref, f32[1,1024]{1,0:T(1,128)S(1)} %get-tuple-element.11.weights_ref), custom_call_target="tpu_custom_call" | custom-call | tf_op jit(solution)/shard_map/pallas_call | solution.py:276
  62.9 12.4 %all_to_all.38.refs_1_ = f32[16,1,1536]{2,1,0:T(1,128)S(1)} all-to-all(f32[16,1,1536]{2,1,0:T(1,128)S(1)} %shard_map.39), channel_id=1, replica_groups=mesh['y'=8,'core'=2,'z'=8,'x'=4] {'y','core'}, dimensions={0} | all-to-all | bytes 196608 | tf_op jit(solution)/shard_map/all_to_all | solution.py:216
  75.2 1.7 %row_kernel.3 = f32[32,1,1024]{2,1,0:T(1,128)S(1)} custom-call(f32[1024,1536]{1,0:T(8,128)S(1)} %get-tuple-element.9.score_ref.refs_0_, f32[16,1,1536]{2,1,0:T(1,128)S(1)} %all_to_all.38.refs_1_), custom_call_target="tpu_custom_call" | custom-call | tf_op jit(solution)/shard_map/row_kernel/pallas_call | solution.py:264
  77.0 13.0 %all_to_all.39.parts_ref = f32[32,1,1024]{2,1,0:T(1,128)S(1)} all-to-all(f32[32,1,1024]{2,1,0:T(1,128)S(1)} %row_kernel.3), channel_id=1, replica_groups=mesh['y'=8,'core'=2,'z'=8,'x'=4] {'z','x'}, dimensions={0} | all-to-all | bytes 262144 | tf_op jit(solution)/shard_map/all_to_all | solution.py:216
  90.0 3.0 %shard_map.40 = f32[2,8,104,128]{3,2,1,0:T(8,128)S(1)} custom-call(f32[1024,1536]{1,0:T(8,128)S(1)} %get-tuple-element.9.score_ref.refs_0_, f32[32,1,1024]{2,1,0:T(1,128)S(1)} %all_to_all.39.parts_ref, f32[1,1024]{1,0:T(1,128)S(1)} %get-tuple-element.11.weights_ref, bf16[128,1024]{1,0:T(8,128)(2,1)S(1)} %get-tuple-element.12.half_ref), custom_call_target="tpu_custom_call" | custom-call | tf_op jit(solution)/shard_map/pallas_call | solution.py:285
  93.0 5.5 %all_to_all.40 = f32[2,8,104,128]{3,2,1,0:T(8,128)S(1)} all-to-all(f32[2,8,104,128]{3,2,1,0:T(8,128)S(1)} %shard_map.40), channel_id=1, replica_groups=mesh['y'=8,'core'=2,'z'=8,'x'=4] {'core'}, dimensions={0} | all-to-all | bytes 1703936 | tf_op jit(solution)/shard_map/all_to_all | solution.py:216
  98.5 0.3 fusion
  98.8 18.3 %all_to_all.41 = f32[8,104,128]{2,1,0:T(8,128)S(1)} all-to-all(f32[8,104,128]{2,1,0:T(8,128)S(1)} %pad_maximum_fusion), channel_id=1, replica_groups=mesh['y'=8,'core'=2,'z'=8,'x'=4] {'y'}, dimensions={0} | all-to-all | bytes 851968 | tf_op jit(solution)/shard_map/all_to_all | solution.py:216
  117.1 0.2 fusion.1
  117.3 0.7 broadcast_divide_fusion
  (8 shorter events, 0.1 us)

commit v3 on v2

--- a/solution.py
+++ b/solution.py
@@ -63,8 +63,9 @@
 
 def row_group(score_ref, base, pots, spread_ref):
     values = []
-    for tile in range(score_ref.shape[1] // LANES):
-        value = score_ref[pl.ds(base, SUBS), lanes_of(tile)]
+    tiles = score_ref.shape[2] // LANES
+    for tile in range(score_ref.shape[0] * tiles):
+        value = score_ref[tile // tiles, pl.ds(base, SUBS), lanes_of(tile % tiles)]
         values.append(value if pots is None else value + pots[:, lanes_of(tile)])
     spread_ref[pl.ds(base, SUBS), :] = lane_lse(values)
 
@@ -80,11 +81,13 @@
 
 
 def first_kernel(
-    particles_hbm, weights_hbm, targets_hbm,
+    chips, cores, particles_hbm, weights_hbm, targets_hbm,
     score_ref, out_ref, weights_ref, half_ref,
     particles_ref, targets_ref, right_ref, points_sq_ref, spread_ref, sems,
 ):
     rows, size = particles_ref.shape
+    width = targets_ref.shape[0]
+    block = width // (chips * cores)
     scale = LOG2E / (EPS * size)
     copies = [
         pltpu.make_async_copy(targets_hbm, targets_ref, sems.at[0]),
@@ -94,9 +97,16 @@
     for copy in copies:
         copy.start()
     copies[0].wait()
-    for tile in range(targets_ref.shape[0] // LANES):
+    for tile in range(width // LANES):
         lanes = lanes_of(tile)
-        part = targets_ref[lanes, :].T
+        parts, place = [], lanes.start
+        while place < lanes.stop:
+            core, chip = divmod(place // block, chips)
+            count = min(lanes.stop, (place // block + 1) * block) - place
+            start = (chip * cores + core) * block + place % block
+            parts.append(targets_ref[start : start + count, :])
+            place += count
+        part = jnp.concatenate(parts, axis=0).T
         points_sq_ref[:, lanes] = jnp.sum(part * part, axis=0, keepdims=True) * scale
         high, low = split(part)
         for index, half in enumerate((high, low, high, low)):
@@ -113,7 +123,9 @@
         high, low = split(source * (2.0 * scale))
         left = jnp.concatenate([high, high, low, low], axis=1)
         cross = jnp.dot(left, right_ref[...], preferred_element_type=jnp.float32)
-        score_ref[part, :] = cross - source_sq - points_sq
+        cross = cross - source_sq - points_sq
+        for core in range(cores):
+            score_ref[core, part, :] = cross[:, core * width // cores : (core + 1) * width // cores]
         half_ref[:, part] = source.T.astype(jnp.bfloat16)
 
     def partials(index):
@@ -136,12 +148,12 @@
         row_group(score_ref, pl.multiple_of(group * SUBS, SUBS), pots, spread_ref)
         return carry
 
-    lax.fori_loop(0, score_ref.shape[0] // SUBS, body, 0, unroll=8)
+    lax.fori_loop(0, score_ref.shape[1] // SUBS, body, 0, unroll=16)
     send_rows(spread_ref, out_ref)
 
 
 def col_chunk(score_ref, spread_ref, step):
-    base = pl.multiple_of(step * CHUNK, CHUNK)
+    base = step * CHUNK if isinstance(step, int) else pl.multiple_of(step * CHUNK, CHUNK)
     pots = [spread_ref[pl.ds(base + index * SUBS, SUBS), :] for index in range(CHUNK // SUBS)]
     for tile in range(score_ref.shape[1] // LANES):
         yield tile, [
@@ -150,24 +162,25 @@
 
 
 def col_kernel(score_ref, parts_ref, weights_ref, out_ref, spread_ref, chunk_ref):
-    rows, width = score_ref.shape
+    cores, rows, width = score_ref.shape
     row_pot = weights_ref[...] * LOG2E - combine(received(parts_ref))
     spread_rows(row_pot, spread_ref)
 
     def body(step, carry):
-        for tile, values in col_chunk(score_ref, spread_ref, step):
-            chunk_ref[pl.ds(pl.multiple_of(step * SUBS, SUBS), SUBS), lanes_of(tile)] = lane_lse(values)
+        for core in range(cores):
+            for tile, values in col_chunk(score_ref.at[core], spread_ref, step):
+                lanes = lanes_of(core * width // LANES + tile)
+                chunk_ref[pl.ds(pl.multiple_of(step * SUBS, SUBS), SUBS), lanes] = lane_lse(values)
         return carry
 
     lax.fori_loop(0, rows // CHUNK, body, 0)
-    send(out_ref, slice(0, width), combine(chunk_ref[...]))
-
-
-def last_kernel(score_ref, parts_ref, weights_ref, half_ref, out_ref, spread_ref, plan_ref):
+    send(out_ref, slice(0, cores * width), combine(chunk_ref[...]))
+
+
+def half_sums(score_ref, half_ref, spread_ref, out_ref, plan_ref):
     rows, width = score_ref.shape
+    size = half_ref.shape[0]
     tiles = width // LANES
-    row_pot = weights_ref[...] * LOG2E - combine(received(parts_ref))
-    spread_rows(row_pot, spread_ref)
 
     def largest(step, tops):
         news = []
@@ -180,56 +193,71 @@
     )
     top = jnp.concatenate([jnp.max(top, axis=0, keepdims=True) for top in tops], axis=1)
     every = jnp.broadcast_to(top, (SUBS, width))
-
-    def fill(step, totals):
-        news = []
-        for tile, values in col_chunk(score_ref, spread_ref, step):
-            values = [jnp.exp2(value - every[:, lanes_of(tile)]) for value in values]
-            news.append(totals[tile] + tree(jnp.add, values))
-            for index in range(0, len(values), 2):
-                base = pl.multiple_of(step * CHUNK, CHUNK) + index * SUBS
-                plan_ref[pl.ds(base, 2 * SUBS), lanes_of(tile)] = jnp.concatenate(
-                    values[index : index + 2], axis=0
-                ).astype(jnp.bfloat16)
-        return tuple(news)
-
-    totals = lax.fori_loop(
-        0, rows // CHUNK, fill, tuple(jnp.zeros((SUBS, LANES), jnp.float32) for _ in range(tiles))
-    )
+    totals = [jnp.zeros((SUBS, LANES), jnp.float32) for _ in range(tiles)]
+    depth = 2 * CHUNK
+    for part in range(rows // depth):
+        for step in range(part * depth // CHUNK, (part + 1) * depth // CHUNK):
+            for tile, values in col_chunk(score_ref, spread_ref, step):
+                values = [jnp.exp2(value - every[:, lanes_of(tile)]) for value in values]
+                totals[tile] = totals[tile] + tree(jnp.add, values)
+                for index in range(0, len(values), 2):
+                    base = step * CHUNK + index * SUBS
+                    plan_ref[base : base + 2 * SUBS, lanes_of(tile)] = jnp.concatenate(
+                        values[index : index + 2], axis=0
+                    ).astype(jnp.bfloat16)
+        inner = slice(part * depth, (part + 1) * depth)
+        sums = jnp.dot(half_ref[:, inner], plan_ref[inner, :], preferred_element_type=jnp.float32)
+        out_ref[:size, :] = out_ref[:size, :] + sums if part else sums
     total = jnp.concatenate([jnp.sum(total, axis=0, keepdims=True) for total in totals], axis=1)
-    sums = jnp.dot(half_ref[...], plan_ref[...], preferred_element_type=jnp.float32)
-    sums = jnp.concatenate([sums[:, lanes_of(tile)].T for tile in range(tiles)], axis=0)
-    cores, chips, block = out_ref.shape[0], out_ref.shape[1], out_ref.shape[2] - STATS
+    out_ref[size:, :] = jnp.concatenate([top, total, jnp.zeros((STATS - 2, width), jnp.float32)], axis=0)
+
+
+def sibling_kernel(score_ref, parts_ref, weights_ref, half_ref, out_ref, spread_ref, plan_ref):
+    row_pot = weights_ref[...] * LOG2E - combine(received(parts_ref))
+    spread_rows(row_pot, spread_ref)
+    half_sums(score_ref.at[1 - lax.axis_index("core")], half_ref, spread_ref, out_ref, plan_ref)
+
+
+def own_kernel(score_ref, spread_ref, half_ref, out_ref, plan_ref):
+    half_sums(score_ref.at[lax.axis_index("core")], half_ref, spread_ref, out_ref, plan_ref)
+
+
+def join_kernel(own_ref, other_ref, out_ref):
+    chips, block = out_ref.shape[0], out_ref.shape[1] - STATS
+    size = own_ref.shape[0] - STATS
+    tops = [ref[size : size + 1, :] for ref in (own_ref, other_ref)]
+    top = jnp.maximum(*tops)
+    own, other = (jnp.exp2(value - top) for value in tops)
+    total = own_ref[size + 1 : size + 2, :] * own + other_ref[size + 1 : size + 2, :] * other
+    sums = []
+    for tile in range(own_ref.shape[1] // LANES):
+        lanes = lanes_of(tile)
+        sums.append((own_ref[:size, lanes] * own[:, lanes] + other_ref[:size, lanes] * other[:, lanes]).T)
+    sums = jnp.concatenate(sums, axis=0)
     rest = jnp.zeros((1, LANES - block), jnp.float32)
     for chip in range(chips):
-        for core in range(cores):
-            start = (chip * cores + core) * block
-            out_ref[core, chip, :block, :] = sums[start : start + block]
-            for index, row in enumerate((top, total)):
-                out_ref[core, chip, block + index : block + index + 1, :] = jnp.concatenate(
-                    [row[:, start : start + block], rest], axis=1
-                )
-            out_ref[core, chip, block + 2 :, :] = jnp.zeros((STATS - 2, LANES), jnp.float32)
+        part = slice(chip * block, (chip + 1) * block)
+        out_ref[chip, :block, :] = sums[part]
+        stats = [jnp.concatenate([row[:, part], rest], axis=1) for row in (top, total)]
+        out_ref[chip, block:, :] = jnp.concatenate(stats + [jnp.zeros((STATS - 2, LANES), jnp.float32)], axis=0)
+
+
+def final_kernel(blocks_ref, out_ref):
+    chips, block = blocks_ref.shape[0], out_ref.shape[0]
+    tops = [blocks_ref[chip, block : block + 1, :] for chip in range(chips)]
+    top = tree(jnp.maximum, tops)
+    shares = [jnp.exp2(value - top) for value in tops]
+    total = tree(jnp.add, [blocks_ref[chip, block + 1 : block + 2, :] * share for chip, share in enumerate(shares)])
+    scale = 1.0 / jnp.where(total > 0.0, total, 1.0)
+    shares = jnp.concatenate([share * scale for share in shares], axis=0)
+    shares = jnp.concatenate([shares, jnp.zeros((LANES - chips, LANES), jnp.float32)], axis=0).T
+    out_ref[...] = tree(
+        jnp.add, [blocks_ref[chip, :block, :] * shares[:block, chip : chip + 1] for chip in range(chips)]
+    )
 
 
 def exchange(sent, axis):
     return lax.all_to_all(sent, axis, 0, 0, tiled=True)
-
-
-def merge(blocks, block):
-    sums = blocks[..., :block, :]
-    tops = blocks[..., block, :block]
-    totals = blocks[..., block + 1, :block]
-    top = jnp.max(tops, axis=0)
-    weight = jnp.exp2(tops - top[None])
-    return jnp.sum(sums * weight[..., None], axis=0), top, jnp.sum(totals * weight, axis=0)
-
-
-def pack(sums, tops, totals):
-    stats = jnp.stack([tops, totals], axis=-2)
-    pad = [(0, STATS - 2), (0, LANES - tops.shape[-1])]
-    stats = jnp.pad(stats, [(0, 0)] * (stats.ndim - 2) + pad)
-    return jnp.concatenate([sums, stats], axis=-2)
 
 
 def per_device(particles, log_weights, targets):
@@ -245,8 +273,9 @@
     to_rows = f32(chips * cores, 1, width)
 
     score, local, weights, half = pl.pallas_call(
-        first_kernel,
-        out_shape=(f32(rows, width), to_cols, f32(1, rows), jax.ShapeDtypeStruct((size, rows), jnp.bfloat16)),
+        lambda *refs: first_kernel(chips, cores, *refs),
+        name="first_kernel",
+        out_shape=(f32(cores, rows, width // cores), to_cols, f32(1, rows), jax.ShapeDtypeStruct((size, rows), jnp.bfloat16)),
         in_specs=[HBM] * 3,
         out_specs=(VMEM,) * 4,
         scratch_shapes=[
@@ -282,18 +311,45 @@
             compiler_params=params,
         )(score, parts, weights)
         parts = exchange(local, row_axes)
+    part = f32(size + STATS, width // cores)
+    plan = pltpu.VMEM((rows, width // cores), jnp.bfloat16)
+    sent, spreads = pl.pallas_call(
+        sibling_kernel,
+        out_shape=(part, f32(rows, LANES)),
+        in_specs=[VMEM] * 4,
+        out_specs=(VMEM,) * 2,
+        scratch_shapes=[plan],
+        compiler_params=params,
+    )(score, parts, weights, half)
+    other = lax.ppermute(sent, "core", [(core, (core + 1) % cores) for core in range(cores)])
+    own = pl.pallas_call(
+        own_kernel,
+        out_shape=part,
+        in_specs=[VMEM] * 3,
+        out_specs=VMEM,
+        scratch_shapes=[plan],
+        compiler_params=params,
+        cost_estimate=pl.CostEstimate(
+            flops=2 * rows * width * size // cores,
+            bytes_accessed=4 * rows * width // cores,
+            transcendentals=rows * width // cores,
+        ),
+    )(score, spreads, half)
     blocks = pl.pallas_call(
-        last_kernel,
-        out_shape=f32(cores, chips, block + STATS, size),
-        in_specs=[VMEM] * 4,
+        join_kernel,
+        out_shape=f32(chips, block + STATS, size),
+        in_specs=[VMEM] * 2,
         out_specs=VMEM,
-        scratch_shapes=[spread, pltpu.VMEM((rows, width), jnp.bfloat16)],
-        compiler_params=params,
-    )(score, parts, weights, half)
-    blocks = exchange(blocks, "core")
-    blocks = exchange(pack(*merge(blocks, block)), "y")
-    sums, _, total = merge(blocks, block)
-    return sums / total[:, None]
+        compiler_params=params,
+    )(own, other)
+    blocks = exchange(blocks, "y")
+    return pl.pallas_call(
+        final_kernel,
+        out_shape=f32(block, size),
+        in_specs=[VMEM],
+        out_specs=VMEM,
+        compiler_params=params,
+    )(blocks)
 
 
 def solution(mesh):

time: 118 us -> 116 us (0.983)
  blocking collectives: 102 us -> 96.9 us
  starting transfers between devices: 0 us -> 3.33 us
  other arithmetic: 1.26 us -> 0 us
    all_to_all x7 -> x6, blocking collectives: 102 us -> 96.9 us  [exchange(): return lax.all_to_all(sent, axis, 0, 0, tiled=True)]
    ppermute x0 -> x1, starting transfers between devices: none -> 3.33 us  [per_device(): lax.ppermute(sent, 'core', [(core, (core + 1) % cores) for core in range(...]
    pallas_call x2 -> x5, Pallas kernels: 7.3 us -> 8.32 us  [the longest x1 4.32 us: per_device(): pl.pallas_call(lambda *refs: first_kernel(chips, cores, *refs), name='fir...]
  transfers between devices with their start and end apart: 0 -> 1, of which waited for: 0 -> 1; matrix products, arithmetic and copies ran while one was open for 0% -> 0% of each run, Pallas kernels for 0% -> 1%
where the time goes in v3:
time: 116 us; the launch traced here: 115 us
  blocking collectives  96.9 us (84%)
  Pallas kernels  14.9 us (13%)
  starting transfers between devices  3.33 us (3%)
    all_to_all x6, blocking collectives, exchange(): return lax.all_to_all(sent, axis, 0, 0, tiled=True)  96.9 us
    pallas_call x1, Pallas kernels, per_device(): pl.pallas_call(lambda *refs: first_kernel(chips, cores, *refs), name='fir...  4.32 us
    pallas_call x2, Pallas kernels, per_device(): pl.pallas_call(col_kernel, out_shape=to_rows, in_specs=[VMEM] * 3, out_sp...  3.53 us
    ppermute x1, starting transfers between devices, per_device(): lax.ppermute(sent, 'core', [(core, (core + 1) % cores) for core in range(...  3.33 us
    pallas_call x2, Pallas kernels, per_device(): pl.pallas_call(lambda *refs: row_kernel(log_count, *refs), name='row_kern...  3.05 us
  transfers between devices with their start and end apart: 1, of which 1 were waited for; matrix products, arithmetic and copies ran while one was open for 0% of the time, Pallas kernels for 1%

profile of v3, /device:TPU:1, one launch (start us, length us, event | category | flops | bytes accessed | tf_op | source)
XLA Modules:
  0.0 115.3 jit_solution(15700689347840496758)
XLA Ops:
  0.0 4.3 %first_kernel.1 = (f32[2,1024,768]{2,1,0:T(8,128)S(1)}, f32[32,1,1024]{2,1,0:T(1,128)S(1)}, f32[1,1024]{1,0:T(1,128)S(1)}, bf16[128,1024]{1,0:T(8,128)(2,1)S(1)}) custom-call(f32[1024,128]{1,0:T(8,128)} %refs_0_.1, f32[1,1024]{1,0:T(1,128)} %bitcast.1, f32[1536,128]{1,0:T(8,128)} %refs_2_.1), custom_call_target="tpu_custom_call" | custom-call | tf_op jit(solution)/shard_map/first_kernel/pallas_call | solution.py:275
  4.3 22.9 %all_to_all.30.parts_ref = f32[32,1,1024]{2,1,0:T(1,128)S(1)} all-to-all(f32[32,1,1024]{2,1,0:T(1,128)S(1)} %get-tuple-element.12), channel_id=1, replica_groups=mesh['y'=8,'core'=2,'z'=8,'x'=4] {'z','x'}, dimensions={0} | all-to-all | bytes 262144 | tf_op jit(solution)/shard_map/all_to_all | solution.py:260
  27.2 1.8 %shard_map.37 = f32[16,1,1536]{2,1,0:T(1,128)S(1)} custom-call(f32[2,1024,768]{2,1,0:T(8,128)S(1)} %get-tuple-element.11.score_ref.refs_0_, f32[32,1,1024]{2,1,0:T(1,128)S(1)} %all_to_all.30.parts_ref, f32[1,1024]{1,0:T(1,128)S(1)} %get-tuple-element.13.weights_ref), custom_call_target="tpu_custom_call" | custom-call | tf_op jit(solution)/shard_map/pallas_call | solution.py:305
  29.0 17.4 %all_to_all.31.refs_1_ = f32[16,1,1536]{2,1,0:T(1,128)S(1)} all-to-all(f32[16,1,1536]{2,1,0:T(1,128)S(1)} %shard_map.37), channel_id=1, replica_groups=mesh['y'=8,'core'=2,'z'=8,'x'=4] {'y','core'}, dimensions={0} | all-to-all | bytes 196608 | tf_op jit(solution)/shard_map/all_to_all | solution.py:260
  46.4 1.5 %row_kernel.2 = f32[32,1,1024]{2,1,0:T(1,128)S(1)} custom-call(f32[2,1024,768]{2,1,0:T(8,128)S(1)} %get-tuple-element.11.score_ref.refs_0_, f32[16,1,1536]{2,1,0:T(1,128)S(1)} %all_to_all.31.refs_1_), custom_call_target="tpu_custom_call" | custom-call | tf_op jit(solution)/shard_map/row_kernel/pallas_call | solution.py:293
  47.9 13.0 %all_to_all.32.parts_ref = f32[32,1,1024]{2,1,0:T(1,128)S(1)} all-to-all(f32[32,1,1024]{2,1,0:T(1,128)S(1)} %row_kernel.2), channel_id=1, replica_groups=mesh['y'=8,'core'=2,'z'=8,'x'=4] {'z','x'}, dimensions={0} | all-to-all | bytes 262144 | tf_op jit(solution)/shard_map/all_to_all | solution.py:260
  60.9 1.8 %shard_map.38 = f32[16,1,1536]{2,1,0:T(1,128)S(1)} custom-call(f32[2,1024,768]{2,1,0:T(8,128)S(1)} %get-tuple-element.11.score_ref.refs_0_, f32[32,1,1024]{2,1,0:T(1,128)S(1)} %all_to_all.32.parts_ref, f32[1,1024]{1,0:T(1,128)S(1)} %get-tuple-element.13.weights_ref), custom_call_target="tpu_custom_call" | custom-call | tf_op jit(solution)/shard_map/pallas_call | solution.py:305
  62.7 12.4 %all_to_all.33.refs_1_ = f32[16,1,1536]{2,1,0:T(1,128)S(1)} all-to-all(f32[16,1,1536]{2,1,0:T(1,128)S(1)} %shard_map.38), channel_id=1, replica_groups=mesh['y'=8,'core'=2,'z'=8,'x'=4] {'y','core'}, dimensions={0} | all-to-all | bytes 196608 | tf_op jit(solution)/shard_map/all_to_all | solution.py:260
  75.1 1.5 %row_kernel.3 = f32[32,1,1024]{2,1,0:T(1,128)S(1)} custom-call(f32[2,1024,768]{2,1,0:T(8,128)S(1)} %get-tuple-element.11.score_ref.refs_0_, f32[16,1,1536]{2,1,0:T(1,128)S(1)} %all_to_all.33.refs_1_), custom_call_target="tpu_custom_call" | custom-call | tf_op jit(solution)/shard_map/row_kernel/pallas_call | solution.py:293
  76.6 13.0 %all_to_all.34.parts_ref = f32[32,1,1024]{2,1,0:T(1,128)S(1)} all-to-all(f32[32,1,1024]{2,1,0:T(1,128)S(1)} %row_kernel.3), channel_id=1, replica_groups=mesh['y'=8,'core'=2,'z'=8,'x'=4] {'z','x'}, dimensions={0} | all-to-all | bytes 262144 | tf_op jit(solution)/shard_map/all_to_all | solution.py:260
  89.6 1.5 %shard_map.39 = (f32[136,768]{1,0:T(8,128)S(1)}, f32[1024,128]{1,0:T(8,128)S(1)}) custom-call(f32[2,1024,768]{2,1,0:T(8,128)S(1)} %get-tuple-element.11.score_ref.refs_0_, f32[32,1,1024]{2,1,0:T(1,128)S(1)} %all_to_all.34.parts_ref, f32[1,1024]{1,0:T(1,128)S(1)} %get-tuple-element.13.weights_ref, bf16[128,1024]{1,0:T(8,128)(2,1)S(1)} %get-tuple-element.14.half_ref), custom_call_target="tpu_custom_call" | custom-call | tf_op jit(solution)/shard_map/pallas_call | solution.py:316
  91.2 3.3 %collective-permute-start = (f32[136,768]{1,0:T(8,128)S(1)}, f32[136,768]{1,0:T(8,128)S(1)}, u32[]{:S(2)}, u32[]{:S(2)}) collective-permute-start(f32[136,768]{1,0:T(8,128)S(1)} %get-tuple-element.16), channel_id=1, source_target_pairs={{0,32},{32,0},{1,33},{33,1},{2,34},{34,2},{3,35},{35,3},{4,36},{36... | collective-permute-start | bytes 1253384 | tf_op jit(solution)/shard_map/ppermute | solution.py:324
  94.5 1.3 %shard_map.40.own_ref = f32[136,768]{1,0:T(8,128)S(1)} custom-call(f32[2,1024,768]{2,1,0:T(8,128)S(1)} %get-tuple-element.11.score_ref.refs_0_, f32[1024,128]{1,0:T(8,128)S(1)} %get-tuple-element.15.spread_ref, bf16[128,1024]{1,0:T(8,128)(2,1)S(1)} %get-tuple-element.14.half_ref), custom_call_target="tpu_custom_call" | custom-call | flops 201326592 | bytes 3145728 | tf_op jit(solution)/shard_map/pallas_call | solution.py:325
  95.8 0.1 collective-permute-done.other_ref
  95.9 0.2 shard_map.41
  96.1 18.3 %all_to_all.35.blocks_ref = f32[8,104,128]{2,1,0:T(8,128)S(1)} all-to-all(f32[8,104,128]{2,1,0:T(8,128)S(1)} %shard_map.41), channel_id=1, replica_groups=mesh['y'=8,'core'=2,'z'=8,'x'=4] {'y'}, dimensions={0} | all-to-all | bytes 851968 | tf_op jit(solution)/shard_map/all_to_all | solution.py:260
  114.4 0.9 shard_map.42
Async XLA Ops:
  91.2 4.7 %collective-permute-start = (f32[136,768]{1,0:T(8,128)S(1)}, f32[136,768]{1,0:T(8,128)S(1)}, u32[]{:S(2)}, u32[]{:S(2)}) collective-permute-start(f32[136,768]{1,0:T(8,128)S(1)} %get-tuple-element.16), channel_id=1, source_target_pairs={{0,32},{32,0},{1,33},{33,1},{2,34},{34,2},{3,35},{35,3},{4,36},{36... | collective-permute-start | bytes 1253384 | tf_op jit(solution)/shard_map/ppermute | solution.py:324

commit v4 on v3

--- a/solution.py
+++ b/solution.py
@@ -62,17 +62,17 @@
 
 
 def row_group(score_ref, base, pots, spread_ref):
+    rows = slice(base, base + SUBS)
     values = []
-    tiles = score_ref.shape[2] // LANES
-    for tile in range(score_ref.shape[0] * tiles):
-        value = score_ref[tile // tiles, pl.ds(base, SUBS), lanes_of(tile % tiles)]
-        values.append(value if pots is None else value + pots[:, lanes_of(tile)])
-    spread_ref[pl.ds(base, SUBS), :] = lane_lse(values)
-
-
-def send_rows(spread_ref, out_ref):
-    for block in range(spread_ref.shape[0] // LANES):
-        send(out_ref, lanes_of(block), combine(spread_ref[lanes_of(block), :].T))
+    for core in range(score_ref.shape[0]):
+        for tile in range(score_ref.shape[2] // LANES):
+            value = score_ref[core, rows, lanes_of(tile)]
+            values.append(value if pots is None else value + pots[core][:, lanes_of(tile)])
+    spread_ref[rows, :] = lane_lse(values)
+
+
+def send_block(spread_ref, out_ref, block):
+    send(out_ref, lanes_of(block), combine(spread_ref[lanes_of(block), :].T))
 
 
 def spread_rows(pot, spread_ref):
@@ -131,49 +131,48 @@
     def partials(index):
         for group in range(step // SUBS):
             row_group(score_ref, index * step + group * SUBS, None, spread_ref)
+        for place in range(index * step // LANES, (index + 1) * step // LANES):
+            send_block(spread_ref, out_ref, place)
 
     for index in range(rows // step):
         scores(index)
         if index:
             partials(index - 1)
     partials(rows // step - 1)
-    send_rows(spread_ref, out_ref)
 
 
 def row_kernel(log_count, score_ref, parts_ref, out_ref, spread_ref):
+    cores, rows, width = score_ref.shape
     col_pot = -log_count - combine(received(parts_ref))
-    pots = jnp.broadcast_to(col_pot, (SUBS, col_pot.shape[1]))
-
-    def body(group, carry):
-        row_group(score_ref, pl.multiple_of(group * SUBS, SUBS), pots, spread_ref)
-        return carry
-
-    lax.fori_loop(0, score_ref.shape[1] // SUBS, body, 0, unroll=16)
-    send_rows(spread_ref, out_ref)
+    pots = jnp.broadcast_to(col_pot, (SUBS, cores * width))
+    pots = [pots[:, core * width : (core + 1) * width] for core in range(cores)]
+    for block in range(rows // LANES):
+        for group in range(LANES // SUBS):
+            row_group(score_ref, block * LANES + group * SUBS, pots, spread_ref)
+        send_block(spread_ref, out_ref, block)
 
 
 def col_chunk(score_ref, spread_ref, step):
-    base = step * CHUNK if isinstance(step, int) else pl.multiple_of(step * CHUNK, CHUNK)
-    pots = [spread_ref[pl.ds(base + index * SUBS, SUBS), :] for index in range(CHUNK // SUBS)]
+    base = step * CHUNK
+    pots = [spread_ref[base + index * SUBS : base + (index + 1) * SUBS, :] for index in range(CHUNK // SUBS)]
     for tile in range(score_ref.shape[1] // LANES):
         yield tile, [
-            score_ref[pl.ds(base + index * SUBS, SUBS), lanes_of(tile)] + pot for index, pot in enumerate(pots)
+            score_ref[base + index * SUBS : base + (index + 1) * SUBS, lanes_of(tile)] + pot for index, pot in enumerate(pots)
         ]
 
 
-def col_kernel(score_ref, parts_ref, weights_ref, out_ref, spread_ref, chunk_ref):
+def col_kernel(score_ref, parts_ref, weights_ref, out_ref, chunk_ref):
     cores, rows, width = score_ref.shape
     row_pot = weights_ref[...] * LOG2E - combine(received(parts_ref))
-    spread_rows(row_pot, spread_ref)
-
-    def body(step, carry):
+    for step in range(rows // CHUNK):
+        spread = jnp.broadcast_to(row_pot[:, lanes_of(step)], (LANES, LANES)).T
         for core in range(cores):
-            for tile, values in col_chunk(score_ref.at[core], spread_ref, step):
+            for tile in range(width // LANES):
+                part = slice(step * CHUNK, (step + 1) * CHUNK)
+                values = score_ref[core, part, lanes_of(tile)] + spread
+                values = [values[index * SUBS : (index + 1) * SUBS] for index in range(CHUNK // SUBS)]
                 lanes = lanes_of(core * width // LANES + tile)
-                chunk_ref[pl.ds(pl.multiple_of(step * SUBS, SUBS), SUBS), lanes] = lane_lse(values)
-        return carry
-
-    lax.fori_loop(0, rows // CHUNK, body, 0)
+                chunk_ref[step * SUBS : (step + 1) * SUBS, lanes] = lane_lse(values)
     send(out_ref, slice(0, cores * width), combine(chunk_ref[...]))
 
 
@@ -182,15 +181,10 @@
     size = half_ref.shape[0]
     tiles = width // LANES
 
-    def largest(step, tops):
-        news = []
+    tops = [jnp.full((SUBS, LANES), LOWEST, jnp.float32) for _ in range(tiles)]
+    for step in range(rows // CHUNK):
         for tile, values in col_chunk(score_ref, spread_ref, step):
-            news.append(jnp.maximum(tops[tile], tree(jnp.maximum, values)))
-        return tuple(news)
-
-    tops = lax.fori_loop(
-        0, rows // CHUNK, largest, tuple(jnp.full((SUBS, LANES), LOWEST, jnp.float32) for _ in range(tiles))
-    )
+            tops[tile] = jnp.maximum(tops[tile], tree(jnp.maximum, values))
     top = jnp.concatenate([jnp.max(top, axis=0, keepdims=True) for top in tops], axis=1)
     every = jnp.broadcast_to(top, (SUBS, width))
     totals = [jnp.zeros((SUBS, LANES), jnp.float32) for _ in range(tiles)]
@@ -307,7 +301,7 @@
             out_shape=to_rows,
             in_specs=[VMEM] * 3,
             out_specs=VMEM,
-            scratch_shapes=[spread, pltpu.VMEM((rows // CHUNK * SUBS, width), jnp.float32)],
+            scratch_shapes=[pltpu.VMEM((rows // CHUNK * SUBS, width), jnp.float32)],
             compiler_params=params,
         )(score, parts, weights)
         parts = exchange(local, row_axes)

time: 116 us -> 115 us (level)
  Pallas kernels: 14.9 us -> 13.7 us
where the time goes in v4:
time: 115 us; the launch traced here: 114 us
  blocking collectives  97 us (84%)
  Pallas kernels  13.7 us (12%)
  starting transfers between devices  3.33 us (3%)
    all_to_all x6, blocking collectives, exchange(): return lax.all_to_all(sent, axis, 0, 0, tiled=True)  97 us
    pallas_call x1, Pallas kernels, per_device(): pl.pallas_call(lambda *refs: first_kernel(chips, cores, *refs), name='fir...  4.29 us
    ppermute x1, starting transfers between devices, per_device(): lax.ppermute(sent, 'core', [(core, (core + 1) % cores) for core in range(...  3.33 us
    pallas_call x2, Pallas kernels, per_device(): pl.pallas_call(col_kernel, out_shape=to_rows, in_specs=[VMEM] * 3, out_sp...  3.09 us
    pallas_call x2, Pallas kernels, per_device(): pl.pallas_call(lambda *refs: row_kernel(log_count, *refs), name='row_kern...  2.49 us
  transfers between devices with their start and end apart: 1, of which 1 were waited for; matrix products, arithmetic and copies ran while one was open for 0% of the time, Pallas kernels for 1%

profile of v4, /device:TPU:1, one launch (start us, length us, event | category | flops | bytes accessed | tf_op | source)
XLA Modules:
  0.0 114.2 jit_solution(313841299757207416)
XLA Ops:
  0.0 4.3 %first_kernel.1 = (f32[2,1024,768]{2,1,0:T(8,128)S(1)}, f32[32,1,1024]{2,1,0:T(1,128)S(1)}, f32[1,1024]{1,0:T(1,128)S(1)}, bf16[128,1024]{1,0:T(8,128)(2,1)S(1)}) custom-call(f32[1024,128]{1,0:T(8,128)} %refs_0_.1, f32[1,1024]{1,0:T(1,128)} %bitcast.1, f32[1536,128]{1,0:T(8,128)} %refs_2_.1), custom_call_target="tpu_custom_call" | custom-call | tf_op jit(solution)/shard_map/first_kernel/pallas_call | solution.py:269
  4.3 22.9 %all_to_all.30.parts_ref = f32[32,1,1024]{2,1,0:T(1,128)S(1)} all-to-all(f32[32,1,1024]{2,1,0:T(1,128)S(1)} %get-tuple-element.12), channel_id=1, replica_groups=mesh['y'=8,'core'=2,'z'=8,'x'=4] {'z','x'}, dimensions={0} | all-to-all | bytes 262144 | tf_op jit(solution)/shard_map/all_to_all | solution.py:254
  27.2 1.5 %shard_map.37 = f32[16,1,1536]{2,1,0:T(1,128)S(1)} custom-call(f32[2,1024,768]{2,1,0:T(8,128)S(1)} %get-tuple-element.11.score_ref.refs_0_, f32[32,1,1024]{2,1,0:T(1,128)S(1)} %all_to_all.30.parts_ref, f32[1,1024]{1,0:T(1,128)S(1)} %get-tuple-element.13.weights_ref), custom_call_target="tpu_custom_call" | custom-call | tf_op jit(solution)/shard_map/pallas_call | solution.py:299
  28.7 17.5 %all_to_all.31.refs_1_ = f32[16,1,1536]{2,1,0:T(1,128)S(1)} all-to-all(f32[16,1,1536]{2,1,0:T(1,128)S(1)} %shard_map.37), channel_id=1, replica_groups=mesh['y'=8,'core'=2,'z'=8,'x'=4] {'y','core'}, dimensions={0} | all-to-all | bytes 196608 | tf_op jit(solution)/shard_map/all_to_all | solution.py:254
  46.2 1.2 %row_kernel.2 = f32[32,1,1024]{2,1,0:T(1,128)S(1)} custom-call(f32[2,1024,768]{2,1,0:T(8,128)S(1)} %get-tuple-element.11.score_ref.refs_0_, f32[16,1,1536]{2,1,0:T(1,128)S(1)} %all_to_all.31.refs_1_), custom_call_target="tpu_custom_call" | custom-call | tf_op jit(solution)/shard_map/row_kernel/pallas_call | solution.py:287
  47.4 13.0 %all_to_all.32.parts_ref = f32[32,1,1024]{2,1,0:T(1,128)S(1)} all-to-all(f32[32,1,1024]{2,1,0:T(1,128)S(1)} %row_kernel.2), channel_id=1, replica_groups=mesh['y'=8,'core'=2,'z'=8,'x'=4] {'z','x'}, dimensions={0} | all-to-all | bytes 262144 | tf_op jit(solution)/shard_map/all_to_all | solution.py:254
  60.4 1.5 %shard_map.38 = f32[16,1,1536]{2,1,0:T(1,128)S(1)} custom-call(f32[2,1024,768]{2,1,0:T(8,128)S(1)} %get-tuple-element.11.score_ref.refs_0_, f32[32,1,1024]{2,1,0:T(1,128)S(1)} %all_to_all.32.parts_ref, f32[1,1024]{1,0:T(1,128)S(1)} %get-tuple-element.13.weights_ref), custom_call_target="tpu_custom_call" | custom-call | tf_op jit(solution)/shard_map/pallas_call | solution.py:299
  62.0 12.4 %all_to_all.33.refs_1_ = f32[16,1,1536]{2,1,0:T(1,128)S(1)} all-to-all(f32[16,1,1536]{2,1,0:T(1,128)S(1)} %shard_map.38), channel_id=1, replica_groups=mesh['y'=8,'core'=2,'z'=8,'x'=4] {'y','core'}, dimensions={0} | all-to-all | bytes 196608 | tf_op jit(solution)/shard_map/all_to_all | solution.py:254
  74.3 1.2 %row_kernel.3 = f32[32,1,1024]{2,1,0:T(1,128)S(1)} custom-call(f32[2,1024,768]{2,1,0:T(8,128)S(1)} %get-tuple-element.11.score_ref.refs_0_, f32[16,1,1536]{2,1,0:T(1,128)S(1)} %all_to_all.33.refs_1_), custom_call_target="tpu_custom_call" | custom-call | tf_op jit(solution)/shard_map/row_kernel/pallas_call | solution.py:287
  75.6 13.0 %all_to_all.34.parts_ref = f32[32,1,1024]{2,1,0:T(1,128)S(1)} all-to-all(f32[32,1,1024]{2,1,0:T(1,128)S(1)} %row_kernel.3), channel_id=1, replica_groups=mesh['y'=8,'core'=2,'z'=8,'x'=4] {'z','x'}, dimensions={0} | all-to-all | bytes 262144 | tf_op jit(solution)/shard_map/all_to_all | solution.py:254
  88.6 1.5 %shard_map.39 = (f32[136,768]{1,0:T(8,128)S(1)}, f32[1024,128]{1,0:T(8,128)S(1)}) custom-call(f32[2,1024,768]{2,1,0:T(8,128)S(1)} %get-tuple-element.11.score_ref.refs_0_, f32[32,1,1024]{2,1,0:T(1,128)S(1)} %all_to_all.34.parts_ref, f32[1,1024]{1,0:T(1,128)S(1)} %get-tuple-element.13.weights_ref, bf16[128,1024]{1,0:T(8,128)(2,1)S(1)} %get-tuple-element.14.half_ref), custom_call_target="tpu_custom_call" | custom-call | tf_op jit(solution)/shard_map/pallas_call | solution.py:310
  90.1 3.3 %collective-permute-start = (f32[136,768]{1,0:T(8,128)S(1)}, f32[136,768]{1,0:T(8,128)S(1)}, u32[]{:S(2)}, u32[]{:S(2)}) collective-permute-start(f32[136,768]{1,0:T(8,128)S(1)} %get-tuple-element.16), channel_id=1, source_target_pairs={{0,32},{32,0},{1,33},{33,1},{2,34},{34,2},{3,35},{35,3},{4,36},{36... | collective-permute-start | bytes 1253384 | tf_op jit(solution)/shard_map/ppermute | solution.py:318
  93.4 1.2 %shard_map.40.own_ref = f32[136,768]{1,0:T(8,128)S(1)} custom-call(f32[2,1024,768]{2,1,0:T(8,128)S(1)} %get-tuple-element.11.score_ref.refs_0_, f32[1024,128]{1,0:T(8,128)S(1)} %get-tuple-element.15.spread_ref, bf16[128,1024]{1,0:T(8,128)(2,1)S(1)} %get-tuple-element.14.half_ref), custom_call_target="tpu_custom_call" | custom-call | flops 201326592 | bytes 3145728 | tf_op jit(solution)/shard_map/pallas_call | solution.py:319
  94.6 0.2 collective-permute-done.other_ref
  94.8 0.2 shard_map.41
  95.0 18.3 %all_to_all.35.blocks_ref = f32[8,104,128]{2,1,0:T(8,128)S(1)} all-to-all(f32[8,104,128]{2,1,0:T(8,128)S(1)} %shard_map.41), channel_id=1, replica_groups=mesh['y'=8,'core'=2,'z'=8,'x'=4] {'y'}, dimensions={0} | all-to-all | bytes 851968 | tf_op jit(solution)/shard_map/all_to_all | solution.py:254
  113.3 0.9 shard_map.42
Async XLA Ops:
  90.1 4.7 %collective-permute-start = (f32[136,768]{1,0:T(8,128)S(1)}, f32[136,768]{1,0:T(8,128)S(1)}, u32[]{:S(2)}, u32[]{:S(2)}) collective-permute-start(f32[136,768]{1,0:T(8,128)S(1)} %get-tuple-element.16), channel_id=1, source_target_pairs={{0,32},{32,0},{1,33},{33,1},{2,34},{34,2},{3,35},{35,3},{4,36},{36... | collective-permute-start | bytes 1253384 | tf_op jit(solution)/shard_map/ppermute | solution.py:318

commit v5 on v4

--- a/solution.py
+++ b/solution.py
@@ -122,10 +122,11 @@
         source_sq = jnp.sum(source * source, axis=1, keepdims=True) * scale
         high, low = split(source * (2.0 * scale))
         left = jnp.concatenate([high, high, low, low], axis=1)
-        cross = jnp.dot(left, right_ref[...], preferred_element_type=jnp.float32)
-        cross = cross - source_sq - points_sq
+        half_width = width // cores
         for core in range(cores):
-            score_ref[core, part, :] = cross[:, core * width // cores : (core + 1) * width // cores]
+            own = slice(core * half_width, (core + 1) * half_width)
+            cross = jnp.dot(left, right_ref[:, own], preferred_element_type=jnp.float32)
+            score_ref[core, part, :] = cross - source_sq - points_sq[:, own]
         half_ref[:, part] = source.T.astype(jnp.bfloat16)
 
     def partials(index):

time: 115 us -> 115 us (level)
  no operation moved by 1% of the time
where the time goes in v5:
time: 115 us; the launch traced here: 114 us
  blocking collectives  97 us (84%)
  Pallas kernels  13.7 us (12%)
  starting transfers between devices  3.33 us (3%)
    all_to_all x6, blocking collectives, exchange(): return lax.all_to_all(sent, axis, 0, 0, tiled=True)  97 us
    pallas_call x1, Pallas kernels, per_device(): pl.pallas_call(lambda *refs: first_kernel(chips, cores, *refs), name='fir...  4.29 us
    ppermute x1, starting transfers between devices, per_device(): lax.ppermute(sent, 'core', [(core, (core + 1) % cores) for core in range(...  3.33 us
    pallas_call x2, Pallas kernels, per_device(): pl.pallas_call(col_kernel, out_shape=to_rows, in_specs=[VMEM] * 3, out_sp...  3.09 us
    pallas_call x2, Pallas kernels, per_device(): pl.pallas_call(lambda *refs: row_kernel(log_count, *refs), name='row_kern...  2.49 us
  transfers between devices with their start and end apart: 1, of which 1 were waited for; matrix products, arithmetic and copies ran while one was open for 0% of the time, Pallas kernels for 1%

profile of v5, /device:TPU:1, one launch (start us, length us, event | category | flops | bytes accessed | tf_op | source)
XLA Modules:
  0.0 114.2 jit_solution(313841299757207416)
XLA Ops:
  0.0 4.3 %first_kernel.1 = (f32[2,1024,768]{2,1,0:T(8,128)S(1)}, f32[32,1,1024]{2,1,0:T(1,128)S(1)}, f32[1,1024]{1,0:T(1,128)S(1)}, bf16[128,1024]{1,0:T(8,128)(2,1)S(1)}) custom-call(f32[1024,128]{1,0:T(8,128)} %refs_0_.1, f32[1,1024]{1,0:T(1,128)} %bitcast.1, f32[1536,128]{1,0:T(8,128)} %refs_2_.1), custom_call_target="tpu_custom_call" | custom-call | tf_op jit(solution)/shard_map/first_kernel/pallas_call | solution.py:270
  4.3 22.9 %all_to_all.30.parts_ref = f32[32,1,1024]{2,1,0:T(1,128)S(1)} all-to-all(f32[32,1,1024]{2,1,0:T(1,128)S(1)} %get-tuple-element.12), channel_id=1, replica_groups=mesh['y'=8,'core'=2,'z'=8,'x'=4] {'z','x'}, dimensions={0} | all-to-all | bytes 262144 | tf_op jit(solution)/shard_map/all_to_all | solution.py:255
  27.2 1.5 %shard_map.37 = f32[16,1,1536]{2,1,0:T(1,128)S(1)} custom-call(f32[2,1024,768]{2,1,0:T(8,128)S(1)} %get-tuple-element.11.score_ref.refs_0_, f32[32,1,1024]{2,1,0:T(1,128)S(1)} %all_to_all.30.parts_ref, f32[1,1024]{1,0:T(1,128)S(1)} %get-tuple-element.13.weights_ref), custom_call_target="tpu_custom_call" | custom-call | tf_op jit(solution)/shard_map/pallas_call | solution.py:300
  28.7 17.5 %all_to_all.31.refs_1_ = f32[16,1,1536]{2,1,0:T(1,128)S(1)} all-to-all(f32[16,1,1536]{2,1,0:T(1,128)S(1)} %shard_map.37), channel_id=1, replica_groups=mesh['y'=8,'core'=2,'z'=8,'x'=4] {'y','core'}, dimensions={0} | all-to-all | bytes 196608 | tf_op jit(solution)/shard_map/all_to_all | solution.py:255
  46.2 1.2 %row_kernel.2 = f32[32,1,1024]{2,1,0:T(1,128)S(1)} custom-call(f32[2,1024,768]{2,1,0:T(8,128)S(1)} %get-tuple-element.11.score_ref.refs_0_, f32[16,1,1536]{2,1,0:T(1,128)S(1)} %all_to_all.31.refs_1_), custom_call_target="tpu_custom_call" | custom-call | tf_op jit(solution)/shard_map/row_kernel/pallas_call | solution.py:288
  47.4 13.0 %all_to_all.32.parts_ref = f32[32,1,1024]{2,1,0:T(1,128)S(1)} all-to-all(f32[32,1,1024]{2,1,0:T(1,128)S(1)} %row_kernel.2), channel_id=1, replica_groups=mesh['y'=8,'core'=2,'z'=8,'x'=4] {'z','x'}, dimensions={0} | all-to-all | bytes 262144 | tf_op jit(solution)/shard_map/all_to_all | solution.py:255
  60.4 1.5 %shard_map.38 = f32[16,1,1536]{2,1,0:T(1,128)S(1)} custom-call(f32[2,1024,768]{2,1,0:T(8,128)S(1)} %get-tuple-element.11.score_ref.refs_0_, f32[32,1,1024]{2,1,0:T(1,128)S(1)} %all_to_all.32.parts_ref, f32[1,1024]{1,0:T(1,128)S(1)} %get-tuple-element.13.weights_ref), custom_call_target="tpu_custom_call" | custom-call | tf_op jit(solution)/shard_map/pallas_call | solution.py:300
  62.0 12.4 %all_to_all.33.refs_1_ = f32[16,1,1536]{2,1,0:T(1,128)S(1)} all-to-all(f32[16,1,1536]{2,1,0:T(1,128)S(1)} %shard_map.38), channel_id=1, replica_groups=mesh['y'=8,'core'=2,'z'=8,'x'=4] {'y','core'}, dimensions={0} | all-to-all | bytes 196608 | tf_op jit(solution)/shard_map/all_to_all | solution.py:255
  74.3 1.2 %row_kernel.3 = f32[32,1,1024]{2,1,0:T(1,128)S(1)} custom-call(f32[2,1024,768]{2,1,0:T(8,128)S(1)} %get-tuple-element.11.score_ref.refs_0_, f32[16,1,1536]{2,1,0:T(1,128)S(1)} %all_to_all.33.refs_1_), custom_call_target="tpu_custom_call" | custom-call | tf_op jit(solution)/shard_map/row_kernel/pallas_call | solution.py:288
  75.6 13.0 %all_to_all.34.parts_ref = f32[32,1,1024]{2,1,0:T(1,128)S(1)} all-to-all(f32[32,1,1024]{2,1,0:T(1,128)S(1)} %row_kernel.3), channel_id=1, replica_groups=mesh['y'=8,'core'=2,'z'=8,'x'=4] {'z','x'}, dimensions={0} | all-to-all | bytes 262144 | tf_op jit(solution)/shard_map/all_to_all | solution.py:255
  88.6 1.5 %shard_map.39 = (f32[136,768]{1,0:T(8,128)S(1)}, f32[1024,128]{1,0:T(8,128)S(1)}) custom-call(f32[2,1024,768]{2,1,0:T(8,128)S(1)} %get-tuple-element.11.score_ref.refs_0_, f32[32,1,1024]{2,1,0:T(1,128)S(1)} %all_to_all.34.parts_ref, f32[1,1024]{1,0:T(1,128)S(1)} %get-tuple-element.13.weights_ref, bf16[128,1024]{1,0:T(8,128)(2,1)S(1)} %get-tuple-element.14.half_ref), custom_call_target="tpu_custom_call" | custom-call | tf_op jit(solution)/shard_map/pallas_call | solution.py:311
  90.1 3.3 %collective-permute-start = (f32[136,768]{1,0:T(8,128)S(1)}, f32[136,768]{1,0:T(8,128)S(1)}, u32[]{:S(2)}, u32[]{:S(2)}) collective-permute-start(f32[136,768]{1,0:T(8,128)S(1)} %get-tuple-element.16), channel_id=1, source_target_pairs={{0,32},{32,0},{1,33},{33,1},{2,34},{34,2},{3,35},{35,3},{4,36},{36... | collective-permute-start | bytes 1253384 | tf_op jit(solution)/shard_map/ppermute | solution.py:319
  93.4 1.2 %shard_map.40.own_ref = f32[136,768]{1,0:T(8,128)S(1)} custom-call(f32[2,1024,768]{2,1,0:T(8,128)S(1)} %get-tuple-element.11.score_ref.refs_0_, f32[1024,128]{1,0:T(8,128)S(1)} %get-tuple-element.15.spread_ref, bf16[128,1024]{1,0:T(8,128)(2,1)S(1)} %get-tuple-element.14.half_ref), custom_call_target="tpu_custom_call" | custom-call | flops 201326592 | bytes 3145728 | tf_op jit(solution)/shard_map/pallas_call | solution.py:320
  94.6 0.2 collective-permute-done.other_ref
  94.8 0.2 shard_map.41
  95.0 18.3 %all_to_all.35.blocks_ref = f32[8,104,128]{2,1,0:T(8,128)S(1)} all-to-all(f32[8,104,128]{2,1,0:T(8,128)S(1)} %shard_map.41), channel_id=1, replica_groups=mesh['y'=8,'core'=2,'z'=8,'x'=4] {'y'}, dimensions={0} | all-to-all | bytes 851968 | tf_op jit(solution)/shard_map/all_to_all | solution.py:255
  113.3 0.9 shard_map.42
Async XLA Ops:
  90.1 4.7 %collective-permute-start = (f32[136,768]{1,0:T(8,128)S(1)}, f32[136,768]{1,0:T(8,128)S(1)}, u32[]{:S(2)}, u32[]{:S(2)}) collective-permute-start(f32[136,768]{1,0:T(8,128)S(1)} %get-tuple-element.16), channel_id=1, source_target_pairs={{0,32},{32,0},{1,33},{33,1},{2,34},{34,2},{3,35},{35,3},{4,36},{36... | collective-permute-start | bytes 1253384 | tf_op jit(solution)/shard_map/ppermute | solution.py:319
